TPU v7x, 512 devices: a whole 4x4x16 slice. The times are simulated.
512 devices in a mesh: row: 16 (over y, x), col: 32 (over z, core).
Axes of the slice: x: 4, y: 4, z: 16, core: 2. Of those that a mesh axis runs over, the one named last changes fastest.
Arguments:
- coords: float32 [3, 16384], replicated, may hold values from 0 to 1
- lengths: float32 [3], replicated, may hold values from 0.4 to 1.2
- pattern: int32 [32, 32], replicated, may hold values from 0 to 1, as said below
- blocks: int32 [32], replicated, may hold values from 0 to 31, each once
- inverses: float32 [2, 512, 512], replicated, as said below
- earlier: bfloat16 [16384, 1024], P('row'), may hold values from -0.29882812 to 0.29882812
Outputs:
- schur: float32 [16384, 16384], P('row', 'col')
Inputs may be any that keep to these rules, and one draw needn't show every extreme that they name: `pattern`: symmetric, with ones on the diagonal. `blocks`: each tile gets its own site block. `inverses`: each of the two factors is lower triangular with a positive diagonal.
All inputs are finite; a program needn't handle non-finite values.
Results may differ from a plain program's by a relative error of at most 0.0007.
Values may be sent and summed in bfloat16 or wider, within the bound.
No kernel may reach another device: no remote copies, remote signals or barrier semaphores. Data moves between devices by JAX's collectives and lax.ppermute only.
A program may use at most 64 MiB of HBM per device.

v0:
```python
import jax
import jax.numpy as jnp
from jax import lax
from jax.experimental import pallas as pl
from jax.experimental.pallas import tpu as pltpu
from jax.sharding import PartitionSpec as P


TB = 512
VM = pl.BlockSpec(memory_space=pltpu.VMEM)
SM = pl.BlockSpec(memory_space=pltpu.SMEM)
HB = pl.BlockSpec(memory_space=pl.ANY)
F32 = jnp.float32
BF16 = jnp.bfloat16


def dot_t(a, b):
    return lax.dot_general(a, b, (((1,), (1,)), ((), ())), preferred_element_type=F32)


def bf(a):
    return a.astype(BF16)


def halves(a):
    high = bf(a)
    return high, bf(a - high.astype(F32))


def dot3(a, b_high, b_low):
    a_high, a_low = halves(a)
    return dot_t(a_high, b_high) + (dot_t(a_low, b_high) + dot_t(a_high, b_low))


def wendland(left, right):
    sq_dist = None
    for component in range(3):
        offset = left[:, component : component + 1] - right[component : component + 1, :]
        sq_dist = offset * offset if sq_dist is None else sq_dist + offset * offset
    radius = jnp.sqrt(sq_dist)
    falloff = jnp.maximum(1.0 - radius, 0.0)
    falloff = falloff * falloff
    return falloff * falloff * (4.0 * radius + 1.0)


def sites(tile, lengths, blocks, coords):
    start = pl.multiple_of(blocks[tile] * TB, TB)
    return jnp.concatenate([coords[c : c + 1, pl.ds(start, TB)] / lengths[c] for c in range(3)], axis=0)


def as_columns(parts):
    return jnp.concatenate([parts, jnp.zeros((5, TB), F32)], axis=0).T


def put(ref, at, to, left, right, kept):
    for s in range(0, TB, 64):
        ref[at + s : at + s + 64, to : to + TB] = wendland(left[s : s + 64], right) * kept.astype(F32)


def panels_kernel(row_tiles_n, row_count):
    def body(ids, lengths, pattern, blocks, coords, inverses, cov_rows, cov_cols, cov_first, inv_high, inv_low):
        panels = [sites(p, lengths, blocks, coords) for p in range(2)]
        for slot in range(row_tiles_n):
            tile = slot * row_count + ids[0]
            left = as_columns(sites(tile, lengths, blocks, coords))
            for p in range(2):
                put(cov_rows, slot * TB, p * TB, left, panels[p], pattern[tile, p])
        left = as_columns(sites(ids[1], lengths, blocks, coords))
        for p in range(2):
            put(cov_cols, 0, p * TB, left, panels[p], pattern[ids[1], p])
        put(cov_first, 0, 0, as_columns(panels[1]), panels[0], pattern[1, 0])
        for p in range(2):
            inv_high[p], inv_low[p] = halves(inverses[p])

    return body


def schur_kernel(row_tiles_n, row_count):
    def body(ids, lengths, pattern, blocks, coords, cov_schur):
        right = sites(ids[1], lengths, blocks, coords)
        for slot in range(row_tiles_n):
            tile = slot * row_count + ids[0]
            left = as_columns(sites(tile, lengths, blocks, coords))
            put(cov_schur, slot * TB, 0, left, right, pattern[tile, ids[1]])

    return body


def fetch(pairs, sems):
    copies = [pltpu.make_async_copy(source, to, sems.at[n]) for n, (source, to) in enumerate(pairs)]
    for copy in copies:
        copy.start()
    return copies


def panel_parts(own, other, panels, core):
    return [(own, panels.at[1 - core]), (other, panels.at[core])]


def rows_kernel(
    ids, own, other, earlier, cov_rows_in, cov_first_in, inv_high_in, inv_low_in, first, second, first_tile,
    panels, rows, cov_rows, cov_first, inv_high, inv_low, sems,
):
    pairs = panel_parts(own, other, panels, ids[2])
    pairs += [(cov_first_in, cov_first), (inv_high_in, inv_high), (inv_low_in, inv_low)]
    pairs += [(earlier, rows), (cov_rows_in, cov_rows)]
    copies = fetch(pairs, sems)
    for copy in copies[:-2]:
        copy.wait()
    zero = panels[0].reshape(TB, -1)
    one = panels[1].reshape(TB, -1)
    inv0 = inv_high[0], inv_low[0]
    inv1 = inv_high[1], inv_low[1]
    tile = bf(dot3(cov_first[...] - dot_t(one, zero), *inv0))
    first_tile[...] = tile
    for copy in copies[-2:]:
        copy.wait()
    for s in range(0, rows.shape[0], TB):
        block = rows[s : s + TB]
        got = bf(dot3(cov_rows[s : s + TB, :TB] - dot_t(block, zero), *inv0))
        first[s : s + TB] = got
        rest = cov_rows[s : s + TB, TB:] - dot_t(block, one) - dot_t(got, tile)
        second[s : s + TB] = bf(dot3(rest, *inv1))


def tail_kernel(chunk):
    def body(
        ids, column_in, own, other, earlier, cov_schur_in, cov_cols_in, inv_high_in, first_in, second_in,
        first_tile_in, out,
        column, panels, rows, cov_schur, cov_cols, inv_high, first, second, first_tile, result, sems, out_sems,
    ):
        pairs = [(column_in, column), (earlier, rows), (cov_schur_in, cov_schur)]
        pairs += panel_parts(own, other, panels, ids[2])
        pairs += [(cov_cols_in, cov_cols), (inv_high_in, inv_high)]
        pairs += [(first_tile_in, first_tile), (first_in, first), (second_in, second)]
        copies = fetch(pairs, sems)
        steps = [pl.ds(s, chunk) for s in range(0, rows.shape[0], chunk)]
        for copy in copies[:3]:
            copy.wait()
        mine = column[...].reshape(TB, -1)
        for at in steps:
            result[at] = cov_schur[at] - dot_t(rows[at], mine)
        for copy in copies[3:-3]:
            copy.wait()
        start = cov_cols[:, :TB] - dot_t(mine, panels[0].reshape(TB, -1))
        rest = cov_cols[:, TB:] - dot_t(mine, panels[1].reshape(TB, -1))
        col_first = bf(dot_t(bf(start), inv_high[0]))
        for copy in copies[-3:]:
            copy.wait()
        rest = rest - dot_t(col_first, first_tile[...])
        col_second = bf(dot_t(bf(rest), inv_high[1]))
        outs = []
        for n, at in enumerate(steps):
            result[at] = result[at] - dot_t(first[at], col_first) - dot_t(second[at], col_second)
            outs.append(pltpu.make_async_copy(result.at[at], out.at[at], out_sems.at[n]))
            outs[-1].start()
        for copy in outs:
            copy.wait()

    return body


def call(body, outs, specs, out_specs=None, limit=63, **kw):
    return pl.pallas_call(
        body,
        out_shape=outs,
        in_specs=specs,
        out_specs=out_specs or [VM] * len(outs),
        compiler_params=pltpu.CompilerParams(vmem_limit_bytes=limit * 1024 * 1024),
        **kw,
    )


def steps(coords, lengths, pattern, blocks, inverses, earlier):
    row_count = lax.axis_size("row")
    col_count = lax.axis_size("col")
    row_index = lax.axis_index("row")
    col_index = lax.axis_index("col")
    core = col_index % 2
    rows_n, width = earlier.shape
    row_tiles_n = rows_n // TB
    piece = TB // row_count
    ids = jnp.stack([row_index, col_index, core]).astype(jnp.int32)

    holder = col_index % row_count
    start = jnp.where(row_index == holder, col_index // row_count * TB, 0)
    mine = lax.dynamic_slice_in_dim(earlier, start, TB, 0).reshape(row_count, piece, width)
    scattered = lax.all_to_all(mine, "row", 0, 0)

    (cov_schur,) = call(
        schur_kernel(row_tiles_n, row_count),
        [jax.ShapeDtypeStruct((rows_n, TB), F32)],
        [SM, SM, SM, SM, VM],
        name="schur",
    )(ids, lengths, pattern, blocks, coords)
    cov_rows, cov_cols, cov_first, inv_high, inv_low = call(
        panels_kernel(row_tiles_n, row_count),
        [
            jax.ShapeDtypeStruct((rows_n, 2 * TB), F32),
            jax.ShapeDtypeStruct((TB, 2 * TB), F32),
            jax.ShapeDtypeStruct((TB, TB), F32),
            jax.ShapeDtypeStruct((2, TB, TB), BF16),
            jax.ShapeDtypeStruct((2, TB, TB), BF16),
        ],
        [SM, SM, SM, SM, VM, VM],
        name="panels",
    )(ids, lengths, pattern, blocks, coords, inverses)
    panel_piece = lax.dynamic_index_in_dim(scattered, 1 - core, 0, keepdims=True)
    column_piece = lax.dynamic_index_in_dim(scattered, holder, 0, keepdims=True)
    panel_piece, column_piece, cov_schur, cov_rows = lax.optimization_barrier(
        (panel_piece, column_piece, cov_schur, cov_rows)
    )
    own = lax.all_to_all(jnp.broadcast_to(panel_piece, scattered.shape), "row", 0, 0)
    other = lax.ppermute(own, "col", [(c, c ^ 1) for c in range(col_count)])
    column = lax.all_to_all(jnp.broadcast_to(column_piece, scattered.shape), "row", 0, 0)
    panels = pltpu.VMEM((2,) + own.shape, BF16)
    square = pltpu.VMEM((TB, TB), BF16)
    pair = pltpu.VMEM((2, TB, TB), BF16)
    tall = pltpu.VMEM((rows_n, TB), BF16)
    whole = pltpu.VMEM(earlier.shape, BF16)
    block = pltpu.VMEM((rows_n, TB), F32)
    wide = pltpu.VMEM((TB, 2 * TB), F32)
    dma = pltpu.SemaphoreType.DMA
    first, second, first_tile = call(
        rows_kernel,
        [
            jax.ShapeDtypeStruct((rows_n, TB), BF16),
            jax.ShapeDtypeStruct((rows_n, TB), BF16),
            jax.ShapeDtypeStruct((TB, TB), BF16),
        ],
        [SM] + [HB] * 7,
        scratch_shapes=[
            panels, whole, pltpu.VMEM((rows_n, 2 * TB), F32), pltpu.VMEM((TB, TB), F32), pair, pair, dma((7,)),
        ],
        name="rows",
    )(ids, own, other, earlier, cov_rows, cov_first, inv_high, inv_low)
    chunk = 256
    return call(
        tail_kernel(chunk),
        jax.ShapeDtypeStruct((rows_n, TB), F32),
        [SM] + [HB] * 10,
        HB,
        scratch_shapes=[
            pltpu.VMEM(column.shape, BF16), panels, whole, block, wide, pair, tall, tall, square, block,
            dma((10,)), dma((rows_n // chunk,)),
        ],
        name="tail",
    )(ids, column, own, other, earlier, cov_schur, cov_cols, inv_high, first, second, first_tile)


def solution(mesh):
    return jax.shard_map(
        steps,
        mesh=mesh,
        in_specs=(P(), P(), P(), P(), P(), P("row", None)),
        out_specs=P("row", "col"),
        check_vma=False,
    )
```

profile of v0, /device:TPU:1, one launch (start us, length us, event | category | flops | bytes accessed | tf_op | source)
XLA Modules:
  0.0 87.1 jit_solution(5616126371460669365)
XLA Ops:
  0.0 2.3 %constant_dynamic-slice_fusion.2 = bf16[512,1024]{1,0:T(8,128)(2,1)} fusion(bf16[1024,1024]{1,0:T(8,128)(2,1)} %earlier.3, s32[]{:T(128)S(6)} %select_n.33), kind=kLoop, calls=%fused_computation.2 | loop fusion | bytes 2097156 | tf_op jit(solution)/shard_map/dynamic_slice | solution.py:187
  2.3 7.6 %all-to-all-start = ((bf16[16,32,1024]{2,1,0:T(8,128)(2,1)}), bf16[16,32,1024]{2,1,0:T(8,128)(2,1)}, u32[]{:S(2)}, u32[]{:S(2)}) async-start(bf16[16,32,1024]{2,1,0:T(8,128)(2,1)} %bitcast.3), calls=%async_computation | async-start | bytes 2097152 | tf_op jit(solution)/shard_map/all_to_all | solution.py:188
  9.9 0.6 pad_add_fusion.ids
  10.5 4.2 %schur.1.cov_schur_in = f32[1024,512]{1,0:T(8,128)} custom-call(s32[3]{0:T(128)} %pad_add_fusion.ids, f32[3]{0:T(128)} %lengths.3, s32[32,32]{1,0:T(8,128)} %pattern.3, s32[32]{0:T(128)} %blocks.3, f32[3,16384]{1,0:T(4,128)} %coords.3), custom_call_target="tpu_custom_call" | custom-call | tf_op jit(solution)/shard_map/schur/pallas_call | solution.py:190
  14.7 10.6 %panels.1 = (f32[1024,1024]{1,0:T(8,128)}, f32[512,1024]{1,0:T(8,128)}, f32[512,512]{1,0:T(8,128)}, bf16[2,512,512]{2,1,0:T(8,128)(2,1)}, bf16[2,512,512]{2,1,0:T(8,128)(2,1)}) custom-call(s32[3]{0:T(128)} %pad_add_fusion.ids, f32[3]{0:T(128)} %lengths.3, s32[32,32]{1,0:T(8,128)} %pattern.3, s32[32]{0:T(128)} %blocks.3, f32[3,16384]{1,0:T(4,128)} %coords.3, ...), custom_call_target="tpu_custom_call" | custom-call | tf_op jit(solution)/shard_map/panels/pallas_call | solution.py:196
  25.3 0.0 all-to-all-done
  25.3 0.9 %constant_dynamic-slice_fusion = (bf16[1,32,1024]{2,1,0:T(8,128)(2,1)S(1)}, bf16[1,32,1024]{2,1,0:T(8,128)(2,1)S(1)}) fusion(bf16[16,32,1024]{2,1,0:T(8,128)(2,1)} %all-to-all-done, s32[]{:T(128)S(6)} %select_n.35, s32[]{:T(128)S(6)} %select_n.34), kind=kLoop, calls=%fused_computation | loop fusion | bytes 262152 | tf_op jit(solution)/shard_map/jit(dynamic_index_in_dim)/dynamic_slice | solution.py:209
  26.2 0.1 broadcast_in_dim.17
  26.3 19.7 %all_to_all.15.own = bf16[16,32,1024]{2,1,0:T(8,128)(2,1)S(1)} all-to-all(bf16[16,32,1024]{2,1,0:T(8,128)(2,1)S(1)} %broadcast_in_dim.17), channel_id=1, replica_groups=mesh['row'=16,'col'=32] {'row'}, dimensions={0} | all-to-all | bytes 2097152 | tf_op jit(solution)/shard_map/all_to_all | solution.py:213
  46.0 0.0 copy-start
  46.0 1.0 %copy-done = bf16[16,32,1024]{2,1,0:T(8,128)(2,1)} copy-done((bf16[16,32,1024]{2,1,0:T(8,128)(2,1)}, bf16[16,32,1024]{2,1,0:T(8,128)(2,1)S(1)}, u32[]{:S(2)}) %copy-start) | copy-done | bytes 1048600
  47.0 6.7 %collective-permute-start = (bf16[16,32,1024]{2,1,0:T(8,128)(2,1)S(1)}, bf16[16,32,1024]{2,1,0:T(8,128)(2,1)S(1)}, u32[]{:S(2)}, u32[]{:S(2)}) collective-permute-start(bf16[16,32,1024]{2,1,0:T(8,128)(2,1)S(1)} %all_to_all.15.own), channel_id=1, source_target_pairs={{0,1},{1,0},{2,3},{3,2},{4,5},{5,4},{6,7},{7,6},{8,9},{9,8},{10,11... | collective-permute-start | bytes 3145736 | tf_op jit(solution)/shard_map/ppermute | solution.py:214
  53.8 1.1 %broadcast_in_dim.15 = bf16[16,32,1024]{2,1,0:T(8,128)(2,1)} broadcast(bf16[32,1024]{1,0:T(8,128)(2,1)S(1)} %bitcast.6), dimensions={1,2} | broadcast | bytes 1114112 | tf_op jit(solution)/shard_map/broadcast_in_dim | solution.py:215
  54.8 4.5 %all-to-all-start.1 = ((bf16[16,32,1024]{2,1,0:T(8,128)(2,1)}), bf16[16,32,1024]{2,1,0:T(8,128)(2,1)}, u32[]{:S(2)}, u32[]{:S(2)}) async-start(bf16[16,32,1024]{2,1,0:T(8,128)(2,1)} %broadcast_in_dim.15), calls=%async_computation.1 | async-start | bytes 2097152 | tf_op jit(solution)/shard_map/all_to_all | solution.py:215
  59.4 0.0 collective-permute-done.other
  59.4 0.0 copy-start.1
  59.4 1.0 %copy-done.1 = bf16[16,32,1024]{2,1,0:T(8,128)(2,1)} copy-done((bf16[16,32,1024]{2,1,0:T(8,128)(2,1)}, bf16[16,32,1024]{2,1,0:T(8,128)(2,1)S(1)}, u32[]{:S(2)}) %copy-start.1) | copy-done | bytes 1048600
  60.4 12.5 %rows.1 = (bf16[1024,512]{1,0:T(8,128)(2,1)}, bf16[1024,512]{1,0:T(8,128)(2,1)}, bf16[512,512]{1,0:T(8,128)(2,1)}) custom-call(s32[3]{0:T(128)} %pad_add_fusion.ids, bf16[16,32,1024]{2,1,0:T(8,128)(2,1)} %copy-done, bf16[16,32,1024]{2,1,0:T(8,128)(2,1)} %copy-done.1, bf16[1024,1024]{1,0:T(8,128)(2,1)} %earlier.3, ...), custom_call_target="tpu_custom_call" | custom-call | tf_op jit(solution)/shard_map/rows/pallas_call | solution.py:224
  72.9 5.1 %all-to-all-done.1.column_in = bf16[16,32,1024]{2,1,0:T(8,128)(2,1)} async-done(((bf16[16,32,1024]{2,1,0:T(8,128)(2,1)}), bf16[16,32,1024]{2,1,0:T(8,128)(2,1)}, u32[]{:S(2)}, u32[]{:S(2)}) %all-to-all-start.1) | async-done | bytes 1048608 | tf_op jit(solution)/shard_map/all_to_all | solution.py:215
  78.0 9.0 %tail.1 = f32[1024,512]{1,0:T(8,128)} custom-call(s32[3]{0:T(128)} %pad_add_fusion.ids, bf16[16,32,1024]{2,1,0:T(8,128)(2,1)} %all-to-all-done.1.column_in, bf16[16,32,1024]{2,1,0:T(8,128)(2,1)} %copy-done, bf16[16,32,1024]{2,1,0:T(8,128)(2,1)} %copy-done.1, bf16[1024,1024]{1,0:T(8,128)(2,1)} %earlier.3, f32[1024,512]{1,0:T(8,128)} %schur.1.cov_schur_in, ...), custom_call_target="tpu_custom_call" | custom-call | tf_op jit(solution)/shard_map/tail/pallas_call | solution.py:238
Async XLA Ops:
  2.3 23.0 %all-to-all-start = ((bf16[16,32,1024]{2,1,0:T(8,128)(2,1)}), bf16[16,32,1024]{2,1,0:T(8,128)(2,1)}, u32[]{:S(2)}, u32[]{:S(2)}) async-start(bf16[16,32,1024]{2,1,0:T(8,128)(2,1)} %bitcast.3), calls=%async_computation | async-start | bytes 2097152 | tf_op jit(solution)/shard_map/all_to_all | solution.py:188
  46.0 1.0 %copy-start = (bf16[16,32,1024]{2,1,0:T(8,128)(2,1)}, bf16[16,32,1024]{2,1,0:T(8,128)(2,1)S(1)}, u32[]{:S(2)}) copy-start(bf16[16,32,1024]{2,1,0:T(8,128)(2,1)S(1)} %all_to_all.15.own) | copy-start | bytes 3145732
  47.0 12.4 %collective-permute-start = (bf16[16,32,1024]{2,1,0:T(8,128)(2,1)S(1)}, bf16[16,32,1024]{2,1,0:T(8,128)(2,1)S(1)}, u32[]{:S(2)}, u32[]{:S(2)}) collective-permute-start(bf16[16,32,1024]{2,1,0:T(8,128)(2,1)S(1)} %all_to_all.15.own), channel_id=1, source_target_pairs={{0,1},{1,0},{2,3},{3,2},{4,5},{5,4},{6,7},{7,6},{8,9},{9,8},{10,11... | collective-permute-start | bytes 3145736 | tf_op jit(solution)/shard_map/ppermute | solution.py:214
  54.8 23.2 %all-to-all-start.1 = ((bf16[16,32,1024]{2,1,0:T(8,128)(2,1)}), bf16[16,32,1024]{2,1,0:T(8,128)(2,1)}, u32[]{:S(2)}, u32[]{:S(2)}) async-start(bf16[16,32,1024]{2,1,0:T(8,128)(2,1)} %broadcast_in_dim.15), calls=%async_computation.1 | async-start | bytes 2097152 | tf_op jit(solution)/shard_map/all_to_all | solution.py:215
  59.4 1.0 %copy-start.1 = (bf16[16,32,1024]{2,1,0:T(8,128)(2,1)}, bf16[16,32,1024]{2,1,0:T(8,128)(2,1)S(1)}, u32[]{:S(2)}) copy-start(bf16[16,32,1024]{2,1,0:T(8,128)(2,1)S(1)} %collective-permute-done.other) | copy-start | bytes 3145732
where the time goes:
time: 87.6 us; the launch traced here: 87.1 us
  Pallas kernels  36.3 us (41%)
  blocking collectives  19.7 us (22%)
  starting transfers between devices  18.9 us (22%)
  local copies, waits for them, and re-layouts  6.33 us (7%)
  waiting for transfers between devices  5.09 us (6%)
    all_to_all x1, blocking collectives, steps(): lax.all_to_all(jnp.broadcast_to(panel_piece, scattered.shape), 'row', 0, 0)  19.7 us
    pallas_call x1, Pallas kernels, steps(): call(rows_kernel, [jax.ShapeDtypeStruct((rows_n, TB), BF16), jax.ShapeDty...  12.5 us
    pallas_call x1, Pallas kernels, steps(): call(panels_kernel(row_tiles_n, row_count), [jax.ShapeDtypeStruct((rows_n...  10.6 us
    pallas_call x1, Pallas kernels, steps(): call(tail_kernel(chunk), jax.ShapeDtypeStruct((rows_n, TB), F32), [SM] +...  8.97 us
    all_to_all x1, starting transfers between devices, steps(): scattered = lax.all_to_all(mine, 'row', 0, 0)  7.62 us
    ppermute x1, starting transfers between devices, steps(): other = lax.ppermute(own, 'col', [(c, c ^ 1) for c in range(col_count)])  6.75 us
    all_to_all x1, waiting for transfers between devices, steps(): lax.all_to_all(jnp.broadcast_to(column_piece, scattered.shape), 'row', 0, 0)  5.09 us
    all_to_all x1, starting transfers between devices, steps(): lax.all_to_all(jnp.broadcast_to(column_piece, scattered.shape), 'row', 0, 0)  4.52 us
  transfers between devices with their start and end apart: 3, of which 1 were waited for; matrix products, arithmetic and copies ran while one was open for 2% of the time, Pallas kernels for 31%

commit v1 on v0

v1 whole, which is shorter than its diff:
```python
import jax
import jax.numpy as jnp
from jax import lax
from jax.experimental import pallas as pl
from jax.experimental.pallas import tpu as pltpu
from jax.sharding import PartitionSpec as P


TB = 512
VM = pl.BlockSpec(memory_space=pltpu.VMEM)
SM = pl.BlockSpec(memory_space=pltpu.SMEM)
HB = pl.BlockSpec(memory_space=pl.ANY)
F32 = jnp.float32
BF16 = jnp.bfloat16


def dot_t(a, b):
    return lax.dot_general(a, b, (((1,), (1,)), ((), ())), preferred_element_type=F32)


def bf(a):
    return a.astype(BF16)


def wendland(left, right):
    sq_dist = None
    for component in range(3):
        offset = left[:, component : component + 1] - right[component : component + 1, :]
        sq_dist = offset * offset if sq_dist is None else sq_dist + offset * offset
    radius = jnp.sqrt(sq_dist)
    falloff = jnp.maximum(1.0 - radius, 0.0)
    falloff = falloff * falloff
    return falloff * falloff * (4.0 * radius + 1.0)


def sites(tile, lengths, blocks, coords):
    start = pl.multiple_of(blocks[tile] * TB, TB)
    return jnp.concatenate([coords[c : c + 1, pl.ds(start, TB)] / lengths[c] for c in range(3)], axis=0)


def as_columns(parts):
    return jnp.concatenate([parts, jnp.zeros((5, TB), F32)], axis=0).T


def put(ref, at, to, left, right, kept):
    for s in range(0, TB, 64):
        ref[at + s : at + s + 64, to : to + TB] = wendland(left[s : s + 64], right) * kept.astype(F32)


def panels_kernel(row_tiles_n, row_count):
    def body(lengths, pattern, blocks, coords, inverses, cov_rows, cov_cols, cov_first, inverse):
        place_row, col_tile = place()
        panels = [sites(p, lengths, blocks, coords) for p in range(2)]
        for slot in range(row_tiles_n):
            tile = slot * row_count + place_row
            left = as_columns(sites(tile, lengths, blocks, coords))
            for p in range(2):
                put(cov_rows, slot * TB, p * TB, left, panels[p], pattern[tile, p])
        left = as_columns(sites(col_tile, lengths, blocks, coords))
        for p in range(2):
            put(cov_cols, 0, p * TB, left, panels[p], pattern[col_tile, p])
        put(cov_first, 0, 0, as_columns(panels[1]), panels[0], pattern[1, 0])
        for p in range(2):
            inverse[p] = bf(inverses[p])

    return body


def schur_kernel(row_tiles_n, row_count):
    def body(lengths, pattern, blocks, coords, cov_schur):
        place_row, col_tile = place()
        right = sites(col_tile, lengths, blocks, coords)
        for slot in range(row_tiles_n):
            tile = slot * row_count + place_row
            left = as_columns(sites(tile, lengths, blocks, coords))
            put(cov_schur, slot * TB, 0, left, right, pattern[tile, col_tile])

    return body


def fetch(pairs, sems):
    copies = [pltpu.make_async_copy(source, to, sems.at[n]) for n, (source, to) in enumerate(pairs)]
    for copy in copies:
        copy.start()
    return copies


def place():
    row = lax.axis_index("row")
    col = lax.axis_index("col")
    return row, col


def pack_kernel(parts):
    def body(earlier, out, sems):
        row, col = place()
        count = out.shape[0]
        start = jnp.where(row == col % count, col // count * count, 0)
        each = count // parts
        pairs = [(earlier.at[pl.ds(start + n * each, each)], out.at[pl.ds(n * each, each)]) for n in range(parts)]
        for copy in fetch(pairs, sems):
            copy.wait()

    return body


def spread_kernel(scattered, out, pieces, sems, out_sems):
    _, col = place()
    count = out.shape[0]
    pairs = [(scattered.at[1 - col % 2], pieces.at[0]), (scattered.at[col % count], pieces.at[1])]
    for copy in fetch(pairs, sems):
        copy.wait()
    for copy in fetch([(pieces, out.at[n]) for n in range(count)], out_sems):
        copy.wait()


def split_kernel(gathered, out, sems):
    each = out.shape[0] // 4
    steps = [pl.ds(n * each, each) for n in range(4)]
    for copy in fetch([(gathered.at[at, 0], out.at[at]) for at in steps], sems):
        copy.wait()


def early_kernel(chunk):
    def body(mine_in, earlier, cov_in, out, mine, rows, cov, result, sems, out_sems):
        steps = [pl.ds(s, chunk) for s in range(0, rows.shape[0], chunk)]
        pairs = [(mine_in.at[:, 1], mine)]
        for at in steps:
            pairs += [(earlier.at[at], rows.at[at]), (cov_in.at[at], cov.at[at])]
        copies = fetch(pairs, sems)
        copies[0].wait()
        column = mine[...].reshape(TB, -1)
        outs = []
        for n, at in enumerate(steps):
            copies[1 + 2 * n].wait()
            copies[2 + 2 * n].wait()
            result[at] = cov[at] - dot_t(rows[at], column)
            outs.append(pltpu.make_async_copy(result.at[at], out.at[at], out_sems.at[n]))
            outs[-1].start()
        for copy in outs:
            copy.wait()

    return body


def final_kernel(chunk):
    def body(
        mine_in, other_in, earlier, early_in, cov_rows_in, cov_cols_in, cov_first_in, inverse_in, out,
        mine, panels, rows, early, cov_rows, cov_cols, cov_first, inverse, sems, out_sems,
    ):
        core = place()[1] % 2
        pairs = [(mine_in.at[:, 0], panels.at[1 - core]), (other_in, panels.at[core])]
        pairs += [(mine_in.at[:, 1], mine), (cov_first_in, cov_first), (inverse_in, inverse), (cov_cols_in, cov_cols)]
        steps = [pl.ds(s, chunk) for s in range(0, rows.shape[0], chunk)]
        for at in steps:
            pairs += [(earlier.at[at], rows.at[at]), (cov_rows_in.at[at], cov_rows.at[at])]
        pairs += [(early_in.at[at], early.at[at]) for at in steps]
        copies = fetch(pairs, sems)
        for copy in copies[:3]:
            copy.wait()
        column = mine[...].reshape(TB, -1)
        zero = panels[0].reshape(TB, -1)
        one = panels[1].reshape(TB, -1)
        tile = dot_t(one, zero)
        start = dot_t(column, zero)
        rest = dot_t(column, one)
        for copy in copies[3:6]:
            copy.wait()
        tile = bf(dot_t(bf(cov_first[...] - tile), inverse[0]))
        col_first = bf(dot_t(bf(cov_cols[:, :TB] - start), inverse[0]))
        col_second = bf(dot_t(bf(cov_cols[:, TB:] - rest - dot_t(col_first, tile)), inverse[1]))
        outs = []
        for n, at in enumerate(steps):
            for copy in (*copies[6 + 2 * n : 8 + 2 * n], copies[6 + 2 * len(steps) + n]):
                copy.wait()
            block = rows[at]
            first = bf(dot_t(bf(cov_rows[at, :TB] - dot_t(block, zero)), inverse[0]))
            second = cov_rows[at, TB:] - dot_t(block, one) - dot_t(first, tile)
            second = bf(dot_t(bf(second), inverse[1]))
            early[at] = early[at] - dot_t(first, col_first) - dot_t(second, col_second)
            outs.append(pltpu.make_async_copy(early.at[at], out.at[at], out_sems.at[n]))
            outs[-1].start()
        for copy in outs:
            copy.wait()

    return body


def call(body, outs, specs, out_specs=None, limit=63, **kw):
    return pl.pallas_call(
        body,
        out_shape=outs,
        in_specs=specs,
        out_specs=out_specs or [VM] * len(outs),
        compiler_params=pltpu.CompilerParams(vmem_limit_bytes=limit * 1024 * 1024),
        **kw,
    )


def steps(coords, lengths, pattern, blocks, inverses, earlier):
    row_count = lax.axis_size("row")
    col_count = lax.axis_size("col")
    rows_n, width = earlier.shape
    row_tiles_n = rows_n // TB
    piece = TB // row_count
    dma = pltpu.SemaphoreType.DMA

    pieces = (row_count, piece, width)
    mine = call(pack_kernel(4), jax.ShapeDtypeStruct(pieces, BF16), [HB], HB, scratch_shapes=[dma((4,))], name="pack")(
        earlier.reshape(-1, piece, width)
    )
    scattered = lax.all_to_all(mine, "row", 0, 0)
    (cov_schur,) = call(
        schur_kernel(row_tiles_n, row_count),
        [jax.ShapeDtypeStruct((rows_n, TB), F32)],
        [SM, SM, SM, VM],
        name="schur",
    )(lengths, pattern, blocks, coords)
    scattered, cov_schur, later = lax.optimization_barrier((scattered, cov_schur, lengths))
    spread = call(
        spread_kernel,
        jax.ShapeDtypeStruct((row_count, 2, piece, width), BF16),
        [HB],
        HB,
        63,
        scratch_shapes=[pltpu.VMEM((2, piece, width), BF16), dma((2,)), dma((row_count,))],
        name="spread",
    )(scattered)
    gathered = lax.all_to_all(spread, "row", 0, 0)
    cov_rows, cov_cols, cov_first, inverse = call(
        panels_kernel(row_tiles_n, row_count),
        [
            jax.ShapeDtypeStruct((rows_n, 2 * TB), F32),
            jax.ShapeDtypeStruct((TB, 2 * TB), F32),
            jax.ShapeDtypeStruct((TB, TB), F32),
            jax.ShapeDtypeStruct((2, TB, TB), BF16),
        ],
        [SM, SM, SM, VM, VM],
        name="panels",
    )(later, pattern, blocks, coords, inverses)
    gathered, cov_rows = lax.optimization_barrier((gathered, cov_rows))
    own = call(split_kernel, jax.ShapeDtypeStruct(pieces, BF16), [HB], HB, scratch_shapes=[dma((4,))], name="split")(
        gathered
    )
    other = lax.ppermute(own, "col", [(c, c ^ 1) for c in range(col_count)])
    chunk = 256
    count = rows_n // chunk
    mine_buffer = pltpu.VMEM(pieces, BF16)
    whole = pltpu.VMEM(earlier.shape, BF16)
    block = pltpu.VMEM((rows_n, TB), F32)
    early = call(
        early_kernel(chunk),
        jax.ShapeDtypeStruct((rows_n, TB), F32),
        [HB] * 3,
        HB,
        scratch_shapes=[mine_buffer, whole, block, block, dma((1 + 2 * count,)), dma((count,))],
        name="early",
    )(gathered, earlier, cov_schur)
    other, early = lax.optimization_barrier((other, early))
    return call(
        final_kernel(chunk),
        jax.ShapeDtypeStruct((rows_n, TB), F32),
        [HB] * 8,
        HB,
        scratch_shapes=[
            mine_buffer,
            pltpu.VMEM((2,) + pieces, BF16),
            whole,
            block,
            pltpu.VMEM((rows_n, 2 * TB), F32),
            pltpu.VMEM((TB, 2 * TB), F32),
            pltpu.VMEM((TB, TB), F32),
            pltpu.VMEM((2, TB, TB), BF16),
            dma((6 + 3 * count,)),
            dma((count,)),
        ],
        name="final",
    )(gathered, other, earlier, early, cov_rows, cov_cols, cov_first, inverse)


def solution(mesh):
    return jax.shard_map(
        steps,
        mesh=mesh,
        in_specs=(P(), P(), P(), P(), P(), P("row", None)),
        out_specs=P("row", "col"),
        check_vma=False,
    )
```

time: 87.6 us -> 146 us (1.67)
  the two profiles are of different devices: /device:TPU:1 before, /device:TPU:225 now
where the time goes in v1:
time: 146 us
  Pallas kernels  98.2 us (67%)
  waiting for transfers between devices  28.4 us (19%)
  starting transfers between devices  19 us (13%)
    pallas_call x1, Pallas kernels, steps(): call(split_kernel, jax.ShapeDtypeStruct(pieces, BF16), [HB], HB, scratch_...  32.9 us
    pallas_call x1, Pallas kernels, steps(): call(pack_kernel(4), jax.ShapeDtypeStruct(pieces, BF16), [HB], HB, scratc...  32.9 us
    all_to_all x1, waiting for transfers between devices, steps(): gathered = lax.all_to_all(spread, 'row', 0, 0)  16.4 us
    pallas_call x1, Pallas kernels, steps(): call(final_kernel(chunk), jax.ShapeDtypeStruct((rows_n, TB), F32), [HB] *...  12.4 us
    all_to_all x1, waiting for transfers between devices, steps(): scattered = lax.all_to_all(mine, 'row', 0, 0)  11.9 us
    pallas_call x1, Pallas kernels, steps(): call(panels_kernel(row_tiles_n, row_count), [jax.ShapeDtypeStruct((rows_n...  9.21 us
    ppermute x1, starting transfers between devices, steps(): other = lax.ppermute(own, 'col', [(c, c ^ 1) for c in range(col_count)])  7.76 us
    all_to_all x1, starting transfers between devices, steps(): scattered = lax.all_to_all(mine, 'row', 0, 0)  6.82 us
  transfers between devices with their start and end apart: 3, of which 2 were waited for; matrix products, arithmetic and copies ran while one was open for 0% of the time, Pallas kernels for 12%

profile of v1, /device:TPU:225, one launch (start us, length us, event | category | flops | bytes accessed | tf_op | source)
XLA Modules:
  0.0 145.8 jit_solution(9813025763072601976)
XLA Ops:
  0.0 32.9 %pack.1 = bf16[16,32,1024]{2,1,0:T(8,128)(2,1)} custom-call(bf16[32,32,1024]{2,1,0:T(8,128)(2,1)} %bitcast.1), custom_call_target="tpu_custom_call" | custom-call | tf_op jit(solution)/shard_map/pack/pallas_call | solution.py:209
  32.9 6.8 %all-to-all-start = ((bf16[16,32,1024]{2,1,0:T(8,128)(2,1)}), bf16[16,32,1024]{2,1,0:T(8,128)(2,1)}, u32[]{:S(2)}, u32[]{:S(2)}) async-start(bf16[16,32,1024]{2,1,0:T(8,128)(2,1)} %pack.1), calls=%async_computation | async-start | bytes 2097152 | tf_op jit(solution)/shard_map/all_to_all | solution.py:212
  39.7 4.2 %schur.1.cov_in = f32[1024,512]{1,0:T(8,128)} custom-call(f32[3]{0:T(128)} %lengths.2, s32[32,32]{1,0:T(8,128)} %pattern.3, s32[32]{0:T(128)} %blocks.3, f32[3,16384]{1,0:T(4,128)} %coords.3), custom_call_target="tpu_custom_call" | custom-call | tf_op jit(solution)/shard_map/schur/pallas_call | solution.py:213
  43.9 11.9 %all-to-all-done.scattered = bf16[16,32,1024]{2,1,0:T(8,128)(2,1)} async-done(((bf16[16,32,1024]{2,1,0:T(8,128)(2,1)}), bf16[16,32,1024]{2,1,0:T(8,128)(2,1)}, u32[]{:S(2)}, u32[]{:S(2)}) %all-to-all-start) | async-done | bytes 1048608 | tf_op jit(solution)/shard_map/all_to_all | solution.py:212
  55.8 2.3 %spread.1 = bf16[16,2,32,1024]{3,2,1,0:T(8,128)(2,1)} custom-call(bf16[16,32,1024]{2,1,0:T(8,128)(2,1)} %all-to-all-done.scattered), custom_call_target="tpu_custom_call" | custom-call | tf_op jit(solution)/shard_map/spread/pallas_call | solution.py:220
  58.2 4.5 %all-to-all-start.1 = ((bf16[16,2,32,1024]{3,2,1,0:T(8,128)(2,1)}), bf16[16,2,32,1024]{3,2,1,0:T(8,128)(2,1)}, u32[]{:S(2)}, u32[]{:S(2)}) async-start(bf16[16,2,32,1024]{3,2,1,0:T(8,128)(2,1)} %spread.1), calls=%async_computation.1 | async-start | bytes 4194304 | tf_op jit(solution)/shard_map/all_to_all | solution.py:229
  62.6 9.2 %panels.1 = (f32[1024,1024]{1,0:T(8,128)}, f32[512,1024]{1,0:T(8,128)}, f32[512,512]{1,0:T(8,128)}, bf16[2,512,512]{2,1,0:T(8,128)(2,1)}) custom-call(f32[3]{0:T(128)} %lengths.2, s32[32,32]{1,0:T(8,128)} %pattern.3, s32[32]{0:T(128)} %blocks.3, f32[3,16384]{1,0:T(4,128)} %coords.3, f32[2,512,512]{2,1,0:T(8,128)} %inverses.1), custom_call_target="tpu_custom_call" | custom-call | tf_op jit(solution)/shard_map/panels/pallas_call | solution.py:230
  71.8 16.4 %all-to-all-done.1.gathered.mine_in = bf16[16,2,32,1024]{3,2,1,0:T(8,128)(2,1)} async-done(((bf16[16,2,32,1024]{3,2,1,0:T(8,128)(2,1)}), bf16[16,2,32,1024]{3,2,1,0:T(8,128)(2,1)}, u32[]{:S(2)}, u32[]{:S(2)}) %all-to-all-start.1) | async-done | bytes 2097184 | tf_op jit(solution)/shard_map/all_to_all | solution.py:229
  88.3 32.9 %split.1 = bf16[16,32,1024]{2,1,0:T(8,128)(2,1)} custom-call(bf16[16,2,32,1024]{3,2,1,0:T(8,128)(2,1)} %all-to-all-done.1.gathered.mine_in), custom_call_target="tpu_custom_call" | custom-call | tf_op jit(solution)/shard_map/split/pallas_call | solution.py:242
  121.2 7.8 %collective-permute-start = (bf16[16,32,1024]{2,1,0:T(8,128)(2,1)}, bf16[16,32,1024]{2,1,0:T(8,128)(2,1)}, u32[]{:S(2)}, u32[]{:S(2)}) collective-permute-start(bf16[16,32,1024]{2,1,0:T(8,128)(2,1)} %split.1), channel_id=1, source_target_pairs={{0,1},{1,0},{2,3},{3,2},{4,5},{5,4},{6,7},{7,6},{8,9},{9,8},{10,11... | collective-permute-start | bytes 3145736 | tf_op jit(solution)/shard_map/ppermute | solution.py:245
  129.0 4.3 %early.1.early_in = f32[1024,512]{1,0:T(8,128)} custom-call(bf16[16,2,32,1024]{3,2,1,0:T(8,128)(2,1)} %all-to-all-done.1.gathered.mine_in, bf16[1024,1024]{1,0:T(8,128)(2,1)} %earlier.3, f32[1024,512]{1,0:T(8,128)} %schur.1.cov_in), custom_call_target="tpu_custom_call" | custom-call | tf_op jit(solution)/shard_map/early/pallas_call | solution.py:251
  133.3 0.0 collective-permute-done.other_in
  133.3 12.4 %final.1 = f32[1024,512]{1,0:T(8,128)} custom-call(bf16[16,2,32,1024]{3,2,1,0:T(8,128)(2,1)} %all-to-all-done.1.gathered.mine_in, bf16[16,32,1024]{2,1,0:T(8,128)(2,1)} %collective-permute-done.other_in, bf16[1024,1024]{1,0:T(8,128)(2,1)} %earlier.3, f32[1024,512]{1,0:T(8,128)} %early.1.early_in, f32[1024,1024]{1,0:T(8,128)} %get-tuple-element.23.cov_rows_in, ...), custom_call_target="tpu_custom_call" | custom-call | tf_op jit(solution)/shard_map/final/pallas_call | solution.py:260
Async XLA Ops:
  32.9 22.9 %all-to-all-start = ((bf16[16,32,1024]{2,1,0:T(8,128)(2,1)}), bf16[16,32,1024]{2,1,0:T(8,128)(2,1)}, u32[]{:S(2)}, u32[]{:S(2)}) async-start(bf16[16,32,1024]{2,1,0:T(8,128)(2,1)} %pack.1), calls=%async_computation | async-start | bytes 2097152 | tf_op jit(solution)/shard_map/all_to_all | solution.py:212
  58.2 30.1 %all-to-all-start.1 = ((bf16[16,2,32,1024]{3,2,1,0:T(8,128)(2,1)}), bf16[16,2,32,1024]{3,2,1,0:T(8,128)(2,1)}, u32[]{:S(2)}, u32[]{:S(2)}) async-start(bf16[16,2,32,1024]{3,2,1,0:T(8,128)(2,1)} %spread.1), calls=%async_computation.1 | async-start | bytes 4194304 | tf_op jit(solution)/shard_map/all_to_all | solution.py:229
  121.2 12.1 %collective-permute-start = (bf16[16,32,1024]{2,1,0:T(8,128)(2,1)}, bf16[16,32,1024]{2,1,0:T(8,128)(2,1)}, u32[]{:S(2)}, u32[]{:S(2)}) collective-permute-start(bf16[16,32,1024]{2,1,0:T(8,128)(2,1)} %split.1), channel_id=1, source_target_pairs={{0,1},{1,0},{2,3},{3,2},{4,5},{5,4},{6,7},{7,6},{8,9},{9,8},{10,11... | collective-permute-start | bytes 3145736 | tf_op jit(solution)/shard_map/ppermute | solution.py:245

commit v2 on v1

v2 whole, which is shorter than its diff:
```python
import jax
import jax.numpy as jnp
from jax import lax
from jax.experimental import pallas as pl
from jax.experimental.pallas import tpu as pltpu
from jax.sharding import PartitionSpec as P


TB = 512
VM = pl.BlockSpec(memory_space=pltpu.VMEM)
SM = pl.BlockSpec(memory_space=pltpu.SMEM)
HB = pl.BlockSpec(memory_space=pl.ANY)
F32 = jnp.float32
BF16 = jnp.bfloat16


def dot_t(a, b):
    return lax.dot_general(a, b, (((1,), (1,)), ((), ())), preferred_element_type=F32)


def bf(a):
    return a.astype(BF16)


def wendland(left, right):
    sq_dist = None
    for component in range(3):
        offset = left[:, component : component + 1] - right[component : component + 1, :]
        sq_dist = offset * offset if sq_dist is None else sq_dist + offset * offset
    radius = jnp.sqrt(sq_dist)
    falloff = jnp.maximum(1.0 - radius, 0.0)
    falloff = falloff * falloff
    return falloff * falloff * (4.0 * radius + 1.0)


def sites(tile, lengths, blocks, coords):
    start = pl.multiple_of(blocks[tile] * TB, TB)
    return jnp.concatenate([coords[c : c + 1, pl.ds(start, TB)] / lengths[c] for c in range(3)], axis=0)


def as_columns(parts):
    return jnp.concatenate([parts, jnp.zeros((5, TB), F32)], axis=0).T


def put(ref, at, to, left, right, kept):
    for s in range(0, TB, 64):
        ref[at + s : at + s + 64, to : to + TB] = wendland(left[s : s + 64], right) * kept.astype(F32)


def panels_kernel(row_tiles_n, row_count):
    def body(lengths, pattern, blocks, coords, inverses, cov_rows, cov_cols, cov_first, inverse):
        place_row, col_tile = place()
        panels = [sites(p, lengths, blocks, coords) for p in range(2)]
        for slot in range(row_tiles_n):
            tile = slot * row_count + place_row
            left = as_columns(sites(tile, lengths, blocks, coords))
            for p in range(2):
                put(cov_rows, slot * TB, p * TB, left, panels[p], pattern[tile, p])
        left = as_columns(sites(col_tile, lengths, blocks, coords))
        for p in range(2):
            put(cov_cols, 0, p * TB, left, panels[p], pattern[col_tile, p])
        put(cov_first, 0, 0, as_columns(panels[1]), panels[0], pattern[1, 0])
        for p in range(2):
            inverse[p] = bf(inverses[p])

    return body


def schur_kernel(row_tiles_n, row_count):
    def body(lengths, pattern, blocks, coords, cov_schur):
        place_row, col_tile = place()
        right = sites(col_tile, lengths, blocks, coords)
        for slot in range(row_tiles_n):
            tile = slot * row_count + place_row
            left = as_columns(sites(tile, lengths, blocks, coords))
            put(cov_schur, slot * TB, 0, left, right, pattern[tile, col_tile])

    return body


def fetch(pairs, sems):
    copies = [pltpu.make_async_copy(source, to, sems.at[n]) for n, (source, to) in enumerate(pairs)]
    for copy in copies:
        copy.start()
    return copies


def place():
    row = lax.axis_index("row")
    col = lax.axis_index("col")
    return row, col


def pack_kernel(parts):
    def body(earlier, out, staged, sems, out_sems):
        row, col = place()
        count = out.shape[0]
        start = jnp.where(row == col % count, col // count * count, 0)
        each = count // parts
        steps = [n * each for n in range(parts)]
        copies = fetch([(earlier.at[pl.ds(start + s, each)], staged.at[pl.ds(s, each)]) for s in steps], sems)
        outs = []
        for n, s in enumerate(steps):
            copies[n].wait()
            outs += fetch([(staged.at[pl.ds(s, each)], out.at[pl.ds(s, each)])], out_sems.at[pl.ds(n, 1)])
        for copy in outs:
            copy.wait()

    return body


def spread_kernel(scattered, out, piece, sems, out_sems):
    _, col = place()
    count = out.shape[0]
    for copy in fetch([(scattered.at[col % count], piece)], sems):
        copy.wait()
    for copy in fetch([(piece, out.at[n]) for n in range(count)], out_sems):
        copy.wait()


def times_inverse(block, inverse):
    block = bf(block)
    half = TB // 2
    left = dot_t(block[:, :half], inverse[:half, :half])
    return bf(jnp.concatenate([left, dot_t(block, inverse[half:])], axis=1))


def panel_parts(own, other, panels):
    core = place()[1] % 2
    return [(own, panels.at[1 - core]), (other, panels.at[core])]


def rows_kernel(chunk):
    def body(
        own, other, earlier, cov_rows_in, cov_first_in, inverse_in, first, second, first_tile,
        panels, rows, cov_rows, cov_first, inverse, sems,
    ):
        steps = [pl.ds(s, chunk) for s in range(0, rows.shape[0], chunk)]
        pairs = panel_parts(own, other, panels) + [(cov_first_in, cov_first), (inverse_in, inverse)]
        for at in steps:
            pairs += [(earlier.at[at], rows.at[at]), (cov_rows_in.at[at], cov_rows.at[at])]
        copies = fetch(pairs, sems)
        for copy in copies[:2]:
            copy.wait()
        zero = panels[0].reshape(TB, -1)
        one = panels[1].reshape(TB, -1)
        tile = dot_t(one, zero)
        for copy in copies[2:4]:
            copy.wait()
        tile = times_inverse(cov_first[...] - tile, inverse[0])
        first_tile[...] = tile
        for n, at in enumerate(steps):
            for copy in copies[4 + 2 * n : 6 + 2 * n]:
                copy.wait()
            block = rows[at]
            got = times_inverse(cov_rows[at, :TB] - dot_t(block, zero), inverse[0])
            first[at] = got
            rest = cov_rows[at, TB:] - dot_t(block, one) - dot_t(got, tile)
            second[at] = times_inverse(rest, inverse[1])

    return body


def tail_kernel(chunk):
    def body(
        column_in, own, other, earlier, cov_schur_in, cov_cols_in, inverse_in, first_in, second_in, first_tile_in, out,
        column, panels, rows, cov_schur, cov_cols, inverse, first, second, first_tile, result, sems, out_sems,
    ):
        steps = [pl.ds(s, chunk) for s in range(0, rows.shape[0], chunk)]
        count = len(steps)
        pairs = [(column_in, column)] + [(earlier.at[at], rows.at[at]) for at in steps]
        pairs += panel_parts(own, other, panels) + [(cov_cols_in, cov_cols), (inverse_in, inverse)]
        pairs += [(first_tile_in, first_tile), (first_in, first), (second_in, second), (cov_schur_in, cov_schur)]
        copies = fetch(pairs, sems)
        copies[0].wait()
        mine = column[...].reshape(TB, -1)
        for n, at in enumerate(steps):
            copies[1 + n].wait()
            result[at] = dot_t(rows[at], mine)
        for copy in copies[1 + count : -3]:
            copy.wait()
        start = cov_cols[:, :TB] - dot_t(mine, panels[0].reshape(TB, -1))
        col_first = times_inverse(start, inverse[0])
        rest = cov_cols[:, TB:] - dot_t(mine, panels[1].reshape(TB, -1)) - dot_t(col_first, first_tile[...])
        col_second = times_inverse(rest, inverse[1])
        for copy in copies[-3:]:
            copy.wait()
        outs = []
        for n, at in enumerate(steps):
            result[at] = cov_schur[at] - result[at] - dot_t(first[at], col_first) - dot_t(second[at], col_second)
            outs += fetch([(result.at[at], out.at[at])], out_sems.at[pl.ds(n, 1)])
        for copy in outs:
            copy.wait()

    return body


def call(body, outs, specs, out_specs=None, limit=63, **kw):
    return pl.pallas_call(
        body,
        out_shape=outs,
        in_specs=specs,
        out_specs=out_specs or [VM] * len(outs),
        compiler_params=pltpu.CompilerParams(vmem_limit_bytes=limit * 1024 * 1024),
        **kw,
    )


def steps(coords, lengths, pattern, blocks, inverses, earlier):
    row_count = lax.axis_size("row")
    col_count = lax.axis_size("col")
    rows_n, width = earlier.shape
    row_tiles_n = rows_n // TB
    piece = TB // row_count
    dma = pltpu.SemaphoreType.DMA

    pieces = (row_count, piece, width)
    tile_buffer = pltpu.VMEM(pieces, BF16)
    mine = call(
        pack_kernel(4),
        jax.ShapeDtypeStruct(pieces, BF16),
        [HB],
        HB,
        scratch_shapes=[tile_buffer, dma((4,)), dma((4,))],
        name="pack",
    )(earlier.reshape(-1, piece, width))
    scattered = lax.all_to_all(mine, "row", 0, 0)
    (cov_schur,) = call(
        schur_kernel(row_tiles_n, row_count),
        [jax.ShapeDtypeStruct((rows_n, TB), F32)],
        [SM, SM, SM, VM],
        name="schur",
    )(lengths, pattern, blocks, coords)
    scattered, cov_schur, later = lax.optimization_barrier((scattered, cov_schur, lengths))
    panel_piece = lax.dynamic_index_in_dim(scattered, 1 - lax.axis_index("col") % 2, 0, keepdims=True)
    own = lax.all_to_all(jnp.broadcast_to(panel_piece, pieces), "row", 0, 0)
    spread = call(
        spread_kernel,
        jax.ShapeDtypeStruct(pieces, BF16),
        [HB],
        HB,
        scratch_shapes=[pltpu.VMEM((piece, width), BF16), dma((1,)), dma((row_count,))],
        name="spread",
    )(scattered)
    cov_rows, cov_cols, cov_first, inverse = call(
        panels_kernel(row_tiles_n, row_count),
        [
            jax.ShapeDtypeStruct((rows_n, 2 * TB), F32),
            jax.ShapeDtypeStruct((TB, 2 * TB), F32),
            jax.ShapeDtypeStruct((TB, TB), F32),
            jax.ShapeDtypeStruct((2, TB, TB), BF16),
        ],
        [SM, SM, SM, VM, VM],
        name="panels",
    )(later, pattern, blocks, coords, inverses)
    own, spread, cov_rows = lax.optimization_barrier((own, spread, cov_rows))
    column = lax.all_to_all(spread, "row", 0, 0)
    other = lax.ppermute(own, "col", [(c, c ^ 1) for c in range(col_count)])
    chunk = 256
    count = rows_n // chunk
    panels = pltpu.VMEM((2,) + pieces, BF16)
    square = pltpu.VMEM((TB, TB), BF16)
    pair = pltpu.VMEM((2, TB, TB), BF16)
    tall = pltpu.VMEM((rows_n, TB), BF16)
    whole = pltpu.VMEM(earlier.shape, BF16)
    block = pltpu.VMEM((rows_n, TB), F32)
    first, second, first_tile = call(
        rows_kernel(chunk),
        [
            jax.ShapeDtypeStruct((rows_n, TB), BF16),
            jax.ShapeDtypeStruct((rows_n, TB), BF16),
            jax.ShapeDtypeStruct((TB, TB), BF16),
        ],
        [HB] * 6,
        scratch_shapes=[
            panels, whole, pltpu.VMEM((rows_n, 2 * TB), F32), pltpu.VMEM((TB, TB), F32), pair, dma((4 + 2 * count,)),
        ],
        name="rows",
    )(own, other, earlier, cov_rows, cov_first, inverse)
    return call(
        tail_kernel(chunk),
        jax.ShapeDtypeStruct((rows_n, TB), F32),
        [HB] * 10,
        HB,
        scratch_shapes=[
            tile_buffer, panels, whole, block, pltpu.VMEM((TB, 2 * TB), F32), pair, tall, tall, square, block,
            dma((9 + count,)), dma((count,)),
        ],
        name="tail",
    )(column, own, other, earlier, cov_schur, cov_cols, inverse, first, second, first_tile)


def solution(mesh):
    return jax.shard_map(
        steps,
        mesh=mesh,
        in_specs=(P(), P(), P(), P(), P(), P("row", None)),
        out_specs=P("row", "col"),
        check_vma=False,
    )
```

time: 146 us -> 83.8 us (0.57)
  the two profiles are of different devices: /device:TPU:225 before, /device:TPU:256 now
where the time goes in v2:
time: 83.8 us; the launch traced here: 83.2 us
  Pallas kernels  34.6 us (41%)
  waiting for transfers between devices  28.5 us (34%)
  starting transfers between devices  17.9 us (21%)
  local copies, waits for them, and re-layouts  1.95 us (2%)
    all_to_all x1, waiting for transfers between devices, steps(): scattered = lax.all_to_all(mine, 'row', 0, 0)  13.5 us
    all_to_all x1, waiting for transfers between devices, steps(): column = lax.all_to_all(spread, 'row', 0, 0)  10.2 us
    pallas_call x1, Pallas kernels, steps(): call(rows_kernel(chunk), [jax.ShapeDtypeStruct((rows_n, TB), BF16), jax.S...  9.25 us
    pallas_call x1, Pallas kernels, steps(): call(panels_kernel(row_tiles_n, row_count), [jax.ShapeDtypeStruct((rows_n...  9.23 us
    pallas_call x1, Pallas kernels, steps(): call(tail_kernel(chunk), jax.ShapeDtypeStruct((rows_n, TB), F32), [HB] *...  8.08 us
    all_to_all x1, starting transfers between devices, steps(): scattered = lax.all_to_all(mine, 'row', 0, 0)  7.1 us
    all_to_all x1, waiting for transfers between devices, steps(): own = lax.all_to_all(jnp.broadcast_to(panel_piece, pieces), 'row', 0, 0)  4.74 us
    all_to_all x1, starting transfers between devices, steps(): column = lax.all_to_all(spread, 'row', 0, 0)  4.53 us
  transfers between devices with their start and end apart: 4, of which 3 were waited for; matrix products, arithmetic and copies ran while one was open for 0% of the time, Pallas kernels for 30%

profile of v2, /device:TPU:256, one launch (start us, length us, event | category | flops | bytes accessed | tf_op | source)
XLA Modules:
  0.0 83.2 jit_solution(8106758514730067847)
XLA Ops:
  0.0 2.0 %pack.1 = bf16[16,32,1024]{2,1,0:T(8,128)(2,1)} custom-call(bf16[32,32,1024]{2,1,0:T(8,128)(2,1)} %bitcast.3), custom_call_target="tpu_custom_call" | custom-call | tf_op jit(solution)/shard_map/pack/pallas_call | solution.py:219
  2.0 7.1 %all-to-all-start = ((bf16[16,32,1024]{2,1,0:T(8,128)(2,1)}), bf16[16,32,1024]{2,1,0:T(8,128)(2,1)}, u32[]{:S(2)}, u32[]{:S(2)}) async-start(bf16[16,32,1024]{2,1,0:T(8,128)(2,1)} %pack.1), calls=%async_computation | async-start | bytes 2097152 | tf_op jit(solution)/shard_map/all_to_all | solution.py:227
  9.1 4.2 %schur.1.cov_schur_in = f32[1024,512]{1,0:T(8,128)} custom-call(f32[3]{0:T(128)} %lengths.2, s32[32,32]{1,0:T(8,128)} %pattern.3, s32[32]{0:T(128)} %blocks.3, f32[3,16384]{1,0:T(4,128)} %coords.3), custom_call_target="tpu_custom_call" | custom-call | tf_op jit(solution)/shard_map/schur/pallas_call | solution.py:228
  13.3 13.5 %all-to-all-done.scattered = bf16[16,32,1024]{2,1,0:T(8,128)(2,1)} async-done(((bf16[16,32,1024]{2,1,0:T(8,128)(2,1)}), bf16[16,32,1024]{2,1,0:T(8,128)(2,1)}, u32[]{:S(2)}, u32[]{:S(2)}) %all-to-all-start) | async-done | bytes 1048608 | tf_op jit(solution)/shard_map/all_to_all | solution.py:227
  26.8 0.8 %dynamic-slice_bitcast_fusion = bf16[32,1024]{1,0:T(8,128)(2,1)S(1)} fusion(bf16[16,32,1024]{2,1,0:T(8,128)(2,1)} %all-to-all-done.scattered, s32[]{:T(128)S(6)} %select_n.12), kind=kLoop, calls=%fused_computation | loop fusion | bytes 131076 | tf_op jit(solution)/shard_map/broadcast_in_dim | solution.py:236
  27.7 1.1 %broadcast_in_dim.8 = bf16[16,32,1024]{2,1,0:T(8,128)(2,1)} broadcast(bf16[32,1024]{1,0:T(8,128)(2,1)S(1)} %dynamic-slice_bitcast_fusion), dimensions={1,2} | broadcast | bytes 1114112 | tf_op jit(solution)/shard_map/broadcast_in_dim | solution.py:236
  28.8 4.3 %all-to-all-start.1 = ((bf16[16,32,1024]{2,1,0:T(8,128)(2,1)}), bf16[16,32,1024]{2,1,0:T(8,128)(2,1)}, u32[]{:S(2)}, u32[]{:S(2)}) async-start(bf16[16,32,1024]{2,1,0:T(8,128)(2,1)} %broadcast_in_dim.8), calls=%async_computation.1 | async-start | bytes 2097152 | tf_op jit(solution)/shard_map/all_to_all | solution.py:236
  33.1 1.9 %spread.1 = bf16[16,32,1024]{2,1,0:T(8,128)(2,1)} custom-call(bf16[16,32,1024]{2,1,0:T(8,128)(2,1)} %all-to-all-done.scattered), custom_call_target="tpu_custom_call" | custom-call | tf_op jit(solution)/shard_map/spread/pallas_call | solution.py:237
  35.1 9.2 %panels.1 = (f32[1024,1024]{1,0:T(8,128)}, f32[512,1024]{1,0:T(8,128)}, f32[512,512]{1,0:T(8,128)}, bf16[2,512,512]{2,1,0:T(8,128)(2,1)}) custom-call(f32[3]{0:T(128)} %lengths.2, s32[32,32]{1,0:T(8,128)} %pattern.3, s32[32]{0:T(128)} %blocks.3, f32[3,16384]{1,0:T(4,128)} %coords.3, f32[2,512,512]{2,1,0:T(8,128)} %inverses.1), custom_call_target="tpu_custom_call" | custom-call | tf_op jit(solution)/shard_map/panels/pallas_call | solution.py:245
  44.3 4.7 %all-to-all-done.1.own = bf16[16,32,1024]{2,1,0:T(8,128)(2,1)} async-done(((bf16[16,32,1024]{2,1,0:T(8,128)(2,1)}), bf16[16,32,1024]{2,1,0:T(8,128)(2,1)}, u32[]{:S(2)}, u32[]{:S(2)}) %all-to-all-start.1) | async-done | bytes 1048608 | tf_op jit(solution)/shard_map/all_to_all | solution.py:236
  49.0 1.9 %collective-permute-start = (bf16[16,32,1024]{2,1,0:T(8,128)(2,1)}, bf16[16,32,1024]{2,1,0:T(8,128)(2,1)}, u32[]{:S(2)}, u32[]{:S(2)}) collective-permute-start(bf16[16,32,1024]{2,1,0:T(8,128)(2,1)} %all-to-all-done.1.own), channel_id=1, source_target_pairs={{0,1},{1,0},{2,3},{3,2},{4,5},{5,4},{6,7},{7,6},{8,9},{9,8},{10,11... | collective-permute-start | bytes 3145736 | tf_op jit(solution)/shard_map/ppermute | solution.py:258
  51.0 4.5 %all-to-all-start.2 = ((bf16[16,32,1024]{2,1,0:T(8,128)(2,1)}), bf16[16,32,1024]{2,1,0:T(8,128)(2,1)}, u32[]{:S(2)}, u32[]{:S(2)}) async-start(bf16[16,32,1024]{2,1,0:T(8,128)(2,1)} %spread.1), calls=%async_computation.2 | async-start | bytes 2097152 | tf_op jit(solution)/shard_map/all_to_all | solution.py:257
  55.5 0.0 collective-permute-done.other
  55.5 9.2 %rows.1 = (bf16[1024,512]{1,0:T(8,128)(2,1)}, bf16[1024,512]{1,0:T(8,128)(2,1)}, bf16[512,512]{1,0:T(8,128)(2,1)}) custom-call(bf16[16,32,1024]{2,1,0:T(8,128)(2,1)} %all-to-all-done.1.own, bf16[16,32,1024]{2,1,0:T(8,128)(2,1)} %collective-permute-done.other, bf16[1024,1024]{1,0:T(8,128)(2,1)} %earlier.3, f32[1024,1024]{1,0:T(8,128)} %get-tuple-element.26.cov_rows_in, ...), custom_call_target="tpu_custom_call" | custom-call | tf_op jit(solution)/shard_map/rows/pallas_call | solution.py:267
  64.8 10.2 %all-to-all-done.2.column_in = bf16[16,32,1024]{2,1,0:T(8,128)(2,1)} async-done(((bf16[16,32,1024]{2,1,0:T(8,128)(2,1)}), bf16[16,32,1024]{2,1,0:T(8,128)(2,1)}, u32[]{:S(2)}, u32[]{:S(2)}) %all-to-all-start.2) | async-done | bytes 1048608 | tf_op jit(solution)/shard_map/all_to_all | solution.py:257
  75.0 8.1 %tail.1 = f32[1024,512]{1,0:T(8,128)} custom-call(bf16[16,32,1024]{2,1,0:T(8,128)(2,1)} %all-to-all-done.2.column_in, bf16[16,32,1024]{2,1,0:T(8,128)(2,1)} %all-to-all-done.1.own, bf16[16,32,1024]{2,1,0:T(8,128)(2,1)} %collective-permute-done.other, bf16[1024,1024]{1,0:T(8,128)(2,1)} %earlier.3, f32[1024,512]{1,0:T(8,128)} %schur.1.cov_schur_in, ...), custom_call_target="tpu_custom_call" | custom-call | tf_op jit(solution)/shard_map/tail/pallas_call | solution.py:280
Async XLA Ops:
  2.0 24.8 %all-to-all-start = ((bf16[16,32,1024]{2,1,0:T(8,128)(2,1)}), bf16[16,32,1024]{2,1,0:T(8,128)(2,1)}, u32[]{:S(2)}, u32[]{:S(2)}) async-start(bf16[16,32,1024]{2,1,0:T(8,128)(2,1)} %pack.1), calls=%async_computation | async-start | bytes 2097152 | tf_op jit(solution)/shard_map/all_to_all | solution.py:227
  28.8 20.3 %all-to-all-start.1 = ((bf16[16,32,1024]{2,1,0:T(8,128)(2,1)}), bf16[16,32,1024]{2,1,0:T(8,128)(2,1)}, u32[]{:S(2)}, u32[]{:S(2)}) async-start(bf16[16,32,1024]{2,1,0:T(8,128)(2,1)} %broadcast_in_dim.8), calls=%async_computation.1 | async-start | bytes 2097152 | tf_op jit(solution)/shard_map/all_to_all | solution.py:236
  49.0 6.5 %collective-permute-start = (bf16[16,32,1024]{2,1,0:T(8,128)(2,1)}, bf16[16,32,1024]{2,1,0:T(8,128)(2,1)}, u32[]{:S(2)}, u32[]{:S(2)}) collective-permute-start(bf16[16,32,1024]{2,1,0:T(8,128)(2,1)} %all-to-all-done.1.own), channel_id=1, source_target_pairs={{0,1},{1,0},{2,3},{3,2},{4,5},{5,4},{6,7},{7,6},{8,9},{9,8},{10,11... | collective-permute-start | bytes 3145736 | tf_op jit(solution)/shard_map/ppermute | solution.py:258
  51.0 24.0 %all-to-all-start.2 = ((bf16[16,32,1024]{2,1,0:T(8,128)(2,1)}), bf16[16,32,1024]{2,1,0:T(8,128)(2,1)}, u32[]{:S(2)}, u32[]{:S(2)}) async-start(bf16[16,32,1024]{2,1,0:T(8,128)(2,1)} %spread.1), calls=%async_computation.2 | async-start | bytes 2097152 | tf_op jit(solution)/shard_map/all_to_all | solution.py:257

commit v3 on v2

--- a/solution.py
+++ b/solution.py
@@ -47,21 +47,24 @@
         ref[at + s : at + s + 64, to : to + TB] = wendland(left[s : s + 64], right) * kept.astype(F32)
 
 
+def cols_kernel(lengths, pattern, blocks, coords, inverses, cov_cols, inverse):
+    col_tile = place()[1]
+    left = as_columns(sites(col_tile, lengths, blocks, coords))
+    for p in range(2):
+        put(cov_cols, 0, p * TB, left, sites(p, lengths, blocks, coords), pattern[col_tile, p])
+        inverse[p] = bf(inverses[p])
+
+
 def panels_kernel(row_tiles_n, row_count):
-    def body(lengths, pattern, blocks, coords, inverses, cov_rows, cov_cols, cov_first, inverse):
-        place_row, col_tile = place()
+    def body(lengths, pattern, blocks, coords, cov_rows, cov_first):
+        place_row = place()[0]
         panels = [sites(p, lengths, blocks, coords) for p in range(2)]
         for slot in range(row_tiles_n):
             tile = slot * row_count + place_row
             left = as_columns(sites(tile, lengths, blocks, coords))
             for p in range(2):
                 put(cov_rows, slot * TB, p * TB, left, panels[p], pattern[tile, p])
-        left = as_columns(sites(col_tile, lengths, blocks, coords))
-        for p in range(2):
-            put(cov_cols, 0, p * TB, left, panels[p], pattern[col_tile, p])
         put(cov_first, 0, 0, as_columns(panels[1]), panels[0], pattern[1, 0])
-        for p in range(2):
-            inverse[p] = bf(inverses[p])
 
     return body
 
@@ -95,7 +98,8 @@
     def body(earlier, out, staged, sems, out_sems):
         row, col = place()
         count = out.shape[0]
-        start = jnp.where(row == col % count, col // count * count, 0)
+        held = jnp.logical_and(row // 2 == col % count // 2, col >= count + 2)
+        start = jnp.where(held, 2 * count, 0) + col % 2 * count
         each = count // parts
         steps = [n * each for n in range(parts)]
         copies = fetch([(earlier.at[pl.ds(start + s, each)], staged.at[pl.ds(s, each)]) for s in steps], sems)
@@ -109,11 +113,22 @@
     return body
 
 
-def spread_kernel(scattered, out, piece, sems, out_sems):
+def spread_kernel(scattered, exchanged, planed, out, piece, sems, out_sems):
     _, col = place()
     count = out.shape[0]
-    for copy in fetch([(scattered.at[col % count], piece)], sems):
-        copy.wait()
+    core = col % 2
+    clash = col // 2 == count // 2
+
+    @pl.when(clash)
+    def _():
+        for copy in fetch([(planed.at[h], piece.at[h]) for h in range(2)], sems):
+            copy.wait()
+
+    @pl.when(jnp.logical_not(clash))
+    def _():
+        for copy in fetch([(scattered.at[col % count], piece.at[core]), (exchanged.at[0], piece.at[1 - core])], sems):
+            copy.wait()
+
     for copy in fetch([(piece, out.at[n]) for n in range(count)], out_sems):
         copy.wait()
 
@@ -127,7 +142,10 @@
 
 def panel_parts(own, other, panels):
     core = place()[1] % 2
-    return [(own, panels.at[1 - core]), (other, panels.at[core])]
+    pairs = []
+    for p in range(2):
+        pairs += [(own.at[:, p], panels.at[p, core]), (other.at[:, p], panels.at[p, 1 - core])]
+    return pairs
 
 
 def rows_kernel(chunk):
@@ -140,17 +158,17 @@
         for at in steps:
             pairs += [(earlier.at[at], rows.at[at]), (cov_rows_in.at[at], cov_rows.at[at])]
         copies = fetch(pairs, sems)
-        for copy in copies[:2]:
+        for copy in copies[:4]:
             copy.wait()
         zero = panels[0].reshape(TB, -1)
         one = panels[1].reshape(TB, -1)
         tile = dot_t(one, zero)
-        for copy in copies[2:4]:
+        for copy in copies[4:6]:
             copy.wait()
         tile = times_inverse(cov_first[...] - tile, inverse[0])
         first_tile[...] = tile
         for n, at in enumerate(steps):
-            for copy in copies[4 + 2 * n : 6 + 2 * n]:
+            for copy in copies[6 + 2 * n : 8 + 2 * n]:
                 copy.wait()
             block = rows[at]
             got = times_inverse(cov_rows[at, :TB] - dot_t(block, zero), inverse[0])
@@ -168,16 +186,18 @@
     ):
         steps = [pl.ds(s, chunk) for s in range(0, rows.shape[0], chunk)]
         count = len(steps)
-        pairs = [(column_in, column)] + [(earlier.at[at], rows.at[at]) for at in steps]
+        pairs = [(column_in.at[:, h], column.at[h]) for h in range(2)]
+        pairs += [(earlier.at[at], rows.at[at]) for at in steps]
         pairs += panel_parts(own, other, panels) + [(cov_cols_in, cov_cols), (inverse_in, inverse)]
         pairs += [(first_tile_in, first_tile), (first_in, first), (second_in, second), (cov_schur_in, cov_schur)]
         copies = fetch(pairs, sems)
-        copies[0].wait()
+        for copy in copies[:2]:
+            copy.wait()
         mine = column[...].reshape(TB, -1)
         for n, at in enumerate(steps):
-            copies[1 + n].wait()
+            copies[2 + n].wait()
             result[at] = dot_t(rows[at], mine)
-        for copy in copies[1 + count : -3]:
+        for copy in copies[2 + count : -3]:
             copy.wait()
         start = cov_cols[:, :TB] - dot_t(mine, panels[0].reshape(TB, -1))
         col_first = times_inverse(start, inverse[0])
@@ -214,51 +234,65 @@
     piece = TB // row_count
     dma = pltpu.SemaphoreType.DMA
 
-    pieces = (row_count, piece, width)
-    tile_buffer = pltpu.VMEM(pieces, BF16)
+    half = piece // 2
+    pieces = (row_count, half, width)
+    both = (row_count, 2, half, width)
+    halves = earlier.reshape(-1, half, width)
     mine = call(
-        pack_kernel(4),
+        pack_kernel(2),
         jax.ShapeDtypeStruct(pieces, BF16),
         [HB],
         HB,
-        scratch_shapes=[tile_buffer, dma((4,)), dma((4,))],
+        scratch_shapes=[pltpu.VMEM(pieces, BF16), dma((2,)), dma((2,))],
         name="pack",
-    )(earlier.reshape(-1, piece, width))
+    )(halves)
     scattered = lax.all_to_all(mine, "row", 0, 0)
+    col_index = lax.axis_index("col")
+    first_col = row_count // 2
+    to_row = jnp.clip(col_index - first_col, 0, row_count - 1)
+    planed = lax.dynamic_slice_in_dim(halves.reshape(2, 2, row_count, half, width)[1], to_row, 1, 1)
+    planed = lax.ppermute(
+        planed,
+        ("row", "col"),
+        [(t * col_count + first_col + r, r * col_count + row_count + t) for t in range(2) for r in range(row_count)],
+    )
     (cov_schur,) = call(
         schur_kernel(row_tiles_n, row_count),
         [jax.ShapeDtypeStruct((rows_n, TB), F32)],
         [SM, SM, SM, VM],
         name="schur",
     )(lengths, pattern, blocks, coords)
-    scattered, cov_schur, later = lax.optimization_barrier((scattered, cov_schur, lengths))
-    panel_piece = lax.dynamic_index_in_dim(scattered, 1 - lax.axis_index("col") % 2, 0, keepdims=True)
-    own = lax.all_to_all(jnp.broadcast_to(panel_piece, pieces), "row", 0, 0)
+    cov_cols, inverse = call(
+        cols_kernel,
+        [jax.ShapeDtypeStruct((TB, 2 * TB), F32), jax.ShapeDtypeStruct((2, TB, TB), BF16)],
+        [SM, SM, SM, VM, VM],
+        name="cols",
+    )(lengths, pattern, blocks, coords, inverses)
+    scattered, cov_schur, cov_cols, later = lax.optimization_barrier((scattered, cov_schur, cov_cols, lengths))
+    own = lax.all_to_all(jnp.broadcast_to(scattered[:2], both), "row", 0, 0)
+    partner = [(c, c ^ 1) for c in range(col_count)]
+    theirs = lax.dynamic_slice_in_dim(scattered, (col_index ^ 1) % row_count, 1, 0)
+    exchanged = lax.ppermute(theirs, "col", partner)
+    cov_rows, cov_first = call(
+        panels_kernel(row_tiles_n, row_count),
+        [jax.ShapeDtypeStruct((rows_n, 2 * TB), F32), jax.ShapeDtypeStruct((TB, TB), F32)],
+        [SM, SM, SM, VM],
+        name="panels",
+    )(later, pattern, blocks, coords)
     spread = call(
         spread_kernel,
-        jax.ShapeDtypeStruct(pieces, BF16),
-        [HB],
+        jax.ShapeDtypeStruct(both, BF16),
+        [HB] * 3,
         HB,
-        scratch_shapes=[pltpu.VMEM((piece, width), BF16), dma((1,)), dma((row_count,))],
+        scratch_shapes=[pltpu.VMEM(both[1:], BF16), dma((2,)), dma((row_count,))],
         name="spread",
-    )(scattered)
-    cov_rows, cov_cols, cov_first, inverse = call(
-        panels_kernel(row_tiles_n, row_count),
-        [
-            jax.ShapeDtypeStruct((rows_n, 2 * TB), F32),
-            jax.ShapeDtypeStruct((TB, 2 * TB), F32),
-            jax.ShapeDtypeStruct((TB, TB), F32),
-            jax.ShapeDtypeStruct((2, TB, TB), BF16),
-        ],
-        [SM, SM, SM, VM, VM],
-        name="panels",
-    )(later, pattern, blocks, coords, inverses)
+    )(scattered, exchanged, planed.reshape(both[1:]))
     own, spread, cov_rows = lax.optimization_barrier((own, spread, cov_rows))
     column = lax.all_to_all(spread, "row", 0, 0)
-    other = lax.ppermute(own, "col", [(c, c ^ 1) for c in range(col_count)])
+    other = lax.ppermute(own, "col", partner)
     chunk = 256
     count = rows_n // chunk
-    panels = pltpu.VMEM((2,) + pieces, BF16)
+    panels = pltpu.VMEM((2, 2) + pieces, BF16)
     square = pltpu.VMEM((TB, TB), BF16)
     pair = pltpu.VMEM((2, TB, TB), BF16)
     tall = pltpu.VMEM((rows_n, TB), BF16)
@@ -273,7 +307,7 @@
         ],
         [HB] * 6,
         scratch_shapes=[
-            panels, whole, pltpu.VMEM((rows_n, 2 * TB), F32), pltpu.VMEM((TB, TB), F32), pair, dma((4 + 2 * count,)),
+            panels, whole, pltpu.VMEM((rows_n, 2 * TB), F32), pltpu.VMEM((TB, TB), F32), pair, dma((6 + 2 * count,)),
         ],
         name="rows",
     )(own, other, earlier, cov_rows, cov_first, inverse)
@@ -283,8 +317,8 @@
         [HB] * 10,
         HB,
         scratch_shapes=[
-            tile_buffer, panels, whole, block, pltpu.VMEM((TB, 2 * TB), F32), pair, tall, tall, square, block,
-            dma((9 + count,)), dma((count,)),
+            pltpu.VMEM((2,) + pieces, BF16), panels, whole, block, pltpu.VMEM((TB, 2 * TB), F32), pair, tall, tall, square, block,
+            dma((12 + count,)), dma((count,)),
         ],
         name="tail",
     )(column, own, other, earlier, cov_schur, cov_cols, inverse, first, second, first_tile)

time: 83.8 us -> 85.5 us (1.020)
  the two profiles are of different devices: /device:TPU:256 before, /device:TPU:128 now
where the time goes in v3:
time: 85.5 us; the launch traced here: 84.9 us
  Pallas kernels  37.3 us (44%)
  starting transfers between devices  31.1 us (36%)
  waiting for transfers between devices  12.4 us (15%)
  local copies, waits for them, and re-layouts  3.74 us (4%)
    all_to_all x1, waiting for transfers between devices, steps(): column = lax.all_to_all(spread, 'row', 0, 0)  10.3 us
    pallas_call x1, Pallas kernels, steps(): call(rows_kernel(chunk), [jax.ShapeDtypeStruct((rows_n, TB), BF16), jax.S...  9.19 us
    ppermute x1, starting transfers between devices, steps(): lax.ppermute(planed, ('row', 'col'), [(t * col_count + first_col + r, r *...  9.08 us
    pallas_call x1, Pallas kernels, steps(): call(tail_kernel(chunk), jax.ShapeDtypeStruct((rows_n, TB), F32), [HB] *...  8.11 us
    all_to_all x1, starting transfers between devices, steps(): scattered = lax.all_to_all(mine, 'row', 0, 0)  7.05 us
    pallas_call x1, Pallas kernels, steps(): call(panels_kernel(row_tiles_n, row_count), [jax.ShapeDtypeStruct((rows_n...  6.91 us
    pallas_call x1, Pallas kernels, steps(): call(cols_kernel, [jax.ShapeDtypeStruct((TB, 2 * TB), F32), jax.ShapeDtyp...  5.25 us
    all_to_all x1, starting transfers between devices, steps(): own = lax.all_to_all(jnp.broadcast_to(scattered[:2], both), 'row', 0, 0)  5.22 us
  transfers between devices with their start and end apart: 6, of which 2 were waited for; matrix products, arithmetic and copies ran while one was open for 2% of the time, Pallas kernels for 32%

profile of v3, /device:TPU:128, one launch (start us, length us, event | category | flops | bytes accessed | tf_op | source)
XLA Modules:
  0.0 84.9 jit_solution(12388550669633190436)
XLA Ops:
  0.0 1.8 %pack.1 = bf16[16,16,1024]{2,1,0:T(8,128)(2,1)} custom-call(bf16[64,16,1024]{2,1,0:T(8,128)(2,1)} %bitcast.5), custom_call_target="tpu_custom_call" | custom-call | tf_op jit(solution)/shard_map/pack/pallas_call | solution.py:241
  1.8 7.0 %all-to-all-start = ((bf16[16,16,1024]{2,1,0:T(8,128)(2,1)}), bf16[16,16,1024]{2,1,0:T(8,128)(2,1)S(1)}, u32[]{:S(2)}, u32[]{:S(2)}) async-start(bf16[16,16,1024]{2,1,0:T(8,128)(2,1)} %pack.1), calls=%async_computation | async-start | bytes 1048576 | tf_op jit(solution)/shard_map/all_to_all | solution.py:249
  8.8 4.2 %schur.1.cov_schur_in = f32[1024,512]{1,0:T(8,128)} custom-call(f32[3]{0:T(128)} %lengths.4, s32[32,32]{1,0:T(8,128)} %pattern.5, s32[32]{0:T(128)} %blocks.5, f32[3,16384]{1,0:T(4,128)} %coords.5), custom_call_target="tpu_custom_call" | custom-call | tf_op jit(solution)/shard_map/schur/pallas_call | solution.py:259
  13.0 5.2 %cols.1 = (f32[512,1024]{1,0:T(8,128)}, bf16[2,512,512]{2,1,0:T(8,128)(2,1)}) custom-call(f32[3]{0:T(128)} %lengths.4, s32[32,32]{1,0:T(8,128)} %pattern.5, s32[32]{0:T(128)} %blocks.5, f32[3,16384]{1,0:T(4,128)} %coords.5, f32[2,512,512]{2,1,0:T(8,128)} %inverses.1), custom_call_target="tpu_custom_call" | custom-call | tf_op jit(solution)/shard_map/cols/pallas_call | solution.py:265
  18.3 0.0 copy-start
  18.3 2.1 %all-to-all-done.scattered = bf16[16,16,1024]{2,1,0:T(8,128)(2,1)S(1)} async-done(((bf16[16,16,1024]{2,1,0:T(8,128)(2,1)}), bf16[16,16,1024]{2,1,0:T(8,128)(2,1)S(1)}, u32[]{:S(2)}, u32[]{:S(2)}) %all-to-all-start) | async-done | bytes 524320 | tf_op jit(solution)/shard_map/all_to_all | solution.py:249
  20.4 0.0 copy-start.1
  20.4 1.2 %broadcast_in_dim.3 = bf16[16,2,16,1024]{3,2,1,0:T(8,128)(2,1)} broadcast(bf16[2,16,1024]{2,1,0:T(8,128)(2,1)S(1)} %slice.7), dimensions={1,2,3} | broadcast | bytes 1114112 | tf_op jit(solution)/shard_map/broadcast_in_dim | solution.py:272
  21.6 5.2 %all-to-all-start.1 = ((bf16[16,2,16,1024]{3,2,1,0:T(8,128)(2,1)}), bf16[16,2,16,1024]{3,2,1,0:T(8,128)(2,1)}, u32[]{:S(2)}, u32[]{:S(2)}) async-start(bf16[16,2,16,1024]{3,2,1,0:T(8,128)(2,1)} %broadcast_in_dim.3), calls=%async_computation.1 | async-start | bytes 2097152 | tf_op jit(solution)/shard_map/all_to_all | solution.py:272
  26.8 0.0 copy-done
  26.8 1.0 %slice.8 = bf16[512,1024]{1,0:T(8,128)(2,1)} slice(bf16[1024,1024]{1,0:T(8,128)(2,1)S(1)} %copy-done), slice={[512:1024], [0:1024]} | slice | bytes 2097152 | tf_op jit(solution)/shard_map/slice | solution.py:253
  27.9 0.8 dynamic-slice_bitcast_fusion
  28.7 9.1 %collective-permute-start.1 = (bf16[2,1,16,1024]{3,2,0,1:T(8,128)(2,1)S(1)}, bf16[2,1,16,1024]{3,2,0,1:T(8,128)(2,1)S(1)}, u32[]{:S(2)}, u32[]{:S(2)}) collective-permute-start(bf16[2,1,16,1024]{3,2,0,1:T(8,128)(2,1)S(1)} %dynamic-slice_bitcast_fusion), channel_id=1, source_target_pairs={{8,16},{9,48},{10,80},{11,112},{12,144},{13,176},{14,208},{15,240}... | collective-permute-start | bytes 196616 | tf_op jit(solution)/shard_map/ppermute | solution.py:254
  37.8 0.0 copy-done.1
  37.9 3.3 %collective-permute-start = (bf16[1,16,1024]{2,1,0:T(8,128)(2,1)S(1)}, bf16[1,16,1024]{2,1,0:T(8,128)(2,1)S(1)}, u32[]{:S(2)}, u32[]{:S(2)}) collective-permute-start(bf16[1,16,1024]{2,1,0:T(8,128)(2,1)S(1)} %constant_dynamic-slice_fusion), channel_id=1, source_target_pairs={{0,1},{1,0},{2,3},{3,2},{4,5},{5,4},{6,7},{7,6},{8,9},{9,8},{10,11... | collective-permute-start | bytes 98312 | tf_op jit(solution)/shard_map/ppermute | solution.py:275
  41.2 6.9 %panels.1 = (f32[1024,1024]{1,0:T(8,128)}, f32[512,512]{1,0:T(8,128)}) custom-call(f32[3]{0:T(128)} %lengths.4, s32[32,32]{1,0:T(8,128)} %pattern.5, s32[32]{0:T(128)} %blocks.5, f32[3,16384]{1,0:T(4,128)} %coords.5), custom_call_target="tpu_custom_call" | custom-call | tf_op jit(solution)/shard_map/panels/pallas_call | solution.py:276
  48.1 0.0 collective-permute-done.1
  48.1 0.0 copy-start.2
  48.1 0.0 collective-permute-done.exchanged
  48.1 0.0 copy-start.3
  48.1 0.6 copy-done.2
  48.7 0.0 copy-done.3
  48.8 1.9 %spread.1 = bf16[16,2,16,1024]{3,2,1,0:T(8,128)(2,1)} custom-call(bf16[16,16,1024]{2,1,0:T(8,128)(2,1)} %copy-done.1, bf16[1,16,1024]{2,1,0:T(8,128)(2,1)} %copy-done.3, bf16[2,16,1024]{2,1,0:T(8,128)(2,1)} %bitcast.7), custom_call_target="tpu_custom_call" | custom-call | tf_op jit(solution)/shard_map/spread/pallas_call | solution.py:282
  50.6 0.0 all-to-all-done.1.own
  50.6 1.9 %collective-permute-start.2 = (bf16[16,2,16,1024]{3,2,1,0:T(8,128)(2,1)}, bf16[16,2,16,1024]{3,2,1,0:T(8,128)(2,1)}, u32[]{:S(2)}, u32[]{:S(2)}) collective-permute-start(bf16[16,2,16,1024]{3,2,1,0:T(8,128)(2,1)} %all-to-all-done.1.own), channel_id=1, source_target_pairs={{0,1},{1,0},{2,3},{3,2},{4,5},{5,4},{6,7},{7,6},{8,9},{9,8},{10,11... | collective-permute-start | bytes 3145736 | tf_op jit(solution)/shard_map/ppermute | solution.py:292
  52.6 4.5 %all-to-all-start.2 = ((bf16[16,2,16,1024]{3,2,1,0:T(8,128)(2,1)}), bf16[16,2,16,1024]{3,2,1,0:T(8,128)(2,1)}, u32[]{:S(2)}, u32[]{:S(2)}) async-start(bf16[16,2,16,1024]{3,2,1,0:T(8,128)(2,1)} %spread.1), calls=%async_computation.2 | async-start | bytes 2097152 | tf_op jit(solution)/shard_map/all_to_all | solution.py:291
  57.1 0.0 collective-permute-done.2.other
  57.1 9.2 %rows.1 = (bf16[1024,512]{1,0:T(8,128)(2,1)}, bf16[1024,512]{1,0:T(8,128)(2,1)}, bf16[512,512]{1,0:T(8,128)(2,1)}) custom-call(bf16[16,2,16,1024]{3,2,1,0:T(8,128)(2,1)} %all-to-all-done.1.own, bf16[16,2,16,1024]{3,2,1,0:T(8,128)(2,1)} %collective-permute-done.2.other, bf16[1024,1024]{1,0:T(8,128)(2,1)} %earlier.3, ...), custom_call_target="tpu_custom_call" | custom-call | tf_op jit(solution)/shard_map/rows/pallas_call | solution.py:301
  66.3 10.3 %all-to-all-done.2.column_in = bf16[16,2,16,1024]{3,2,1,0:T(8,128)(2,1)} async-done(((bf16[16,2,16,1024]{3,2,1,0:T(8,128)(2,1)}), bf16[16,2,16,1024]{3,2,1,0:T(8,128)(2,1)}, u32[]{:S(2)}, u32[]{:S(2)}) %all-to-all-start.2) | async-done | bytes 1048608 | tf_op jit(solution)/shard_map/all_to_all | solution.py:291
  76.6 8.1 %tail.1 = f32[1024,512]{1,0:T(8,128)} custom-call(bf16[16,2,16,1024]{3,2,1,0:T(8,128)(2,1)} %all-to-all-done.2.column_in, bf16[16,2,16,1024]{3,2,1,0:T(8,128)(2,1)} %all-to-all-done.1.own, bf16[16,2,16,1024]{3,2,1,0:T(8,128)(2,1)} %collective-permute-done.2.other, bf16[1024,1024]{1,0:T(8,128)(2,1)} %earlier.3, f32[1024,512]{1,0:T(8,128)} %schur.1.cov_schur_in, ...), custom_call_target="tpu_custom_call" | custom-call | tf_op jit(solution)/shard_map/tail/pallas_call | solution.py:314
  (2 shorter events, 0.0 us)
Async XLA Ops:
  1.8 18.6 %all-to-all-start = ((bf16[16,16,1024]{2,1,0:T(8,128)(2,1)}), bf16[16,16,1024]{2,1,0:T(8,128)(2,1)S(1)}, u32[]{:S(2)}, u32[]{:S(2)}) async-start(bf16[16,16,1024]{2,1,0:T(8,128)(2,1)} %pack.1), calls=%async_computation | async-start | bytes 1048576 | tf_op jit(solution)/shard_map/all_to_all | solution.py:249
  18.3 8.6 %copy-start = (bf16[1024,1024]{1,0:T(8,128)(2,1)S(1)}, bf16[1024,1024]{1,0:T(8,128)(2,1)}, u32[]{:S(2)}) copy-start(bf16[1024,1024]{1,0:T(8,128)(2,1)} %earlier.3) | copy-start | bytes 6291460
  20.4 17.5 %copy-start.1 = (bf16[16,16,1024]{2,1,0:T(8,128)(2,1)}, bf16[16,16,1024]{2,1,0:T(8,128)(2,1)S(1)}, u32[]{:S(2)}) copy-start(bf16[16,16,1024]{2,1,0:T(8,128)(2,1)S(1)} %all-to-all-done.scattered) | copy-start | bytes 1572868
  21.6 29.0 %all-to-all-start.1 = ((bf16[16,2,16,1024]{3,2,1,0:T(8,128)(2,1)}), bf16[16,2,16,1024]{3,2,1,0:T(8,128)(2,1)}, u32[]{:S(2)}, u32[]{:S(2)}) async-start(bf16[16,2,16,1024]{3,2,1,0:T(8,128)(2,1)} %broadcast_in_dim.3), calls=%async_computation.1 | async-start | bytes 2097152 | tf_op jit(solution)/shard_map/all_to_all | solution.py:272
  28.7 19.4 %collective-permute-start.1 = (bf16[2,1,16,1024]{3,2,0,1:T(8,128)(2,1)S(1)}, bf16[2,1,16,1024]{3,2,0,1:T(8,128)(2,1)S(1)}, u32[]{:S(2)}, u32[]{:S(2)}) collective-permute-start(bf16[2,1,16,1024]{3,2,0,1:T(8,128)(2,1)S(1)} %dynamic-slice_bitcast_fusion), channel_id=1, source_target_pairs={{8,16},{9,48},{10,80},{11,112},{12,144},{13,176},{14,208},{15,240}... | collective-permute-start | bytes 196616 | tf_op jit(solution)/shard_map/ppermute | solution.py:254
  37.9 10.3 %collective-permute-start = (bf16[1,16,1024]{2,1,0:T(8,128)(2,1)S(1)}, bf16[1,16,1024]{2,1,0:T(8,128)(2,1)S(1)}, u32[]{:S(2)}, u32[]{:S(2)}) collective-permute-start(bf16[1,16,1024]{2,1,0:T(8,128)(2,1)S(1)} %constant_dynamic-slice_fusion), channel_id=1, source_target_pairs={{0,1},{1,0},{2,3},{3,2},{4,5},{5,4},{6,7},{7,6},{8,9},{9,8},{10,11... | collective-permute-start | bytes 98312 | tf_op jit(solution)/shard_map/ppermute | solution.py:275
  48.1 0.6 copy-start.2
  48.1 0.6 copy-start.3
  50.6 6.5 %collective-permute-start.2 = (bf16[16,2,16,1024]{3,2,1,0:T(8,128)(2,1)}, bf16[16,2,16,1024]{3,2,1,0:T(8,128)(2,1)}, u32[]{:S(2)}, u32[]{:S(2)}) collective-permute-start(bf16[16,2,16,1024]{3,2,1,0:T(8,128)(2,1)} %all-to-all-done.1.own), channel_id=1, source_target_pairs={{0,1},{1,0},{2,3},{3,2},{4,5},{5,4},{6,7},{7,6},{8,9},{9,8},{10,11... | collective-permute-start | bytes 3145736 | tf_op jit(solution)/shard_map/ppermute | solution.py:292
  52.6 24.0 %all-to-all-start.2 = ((bf16[16,2,16,1024]{3,2,1,0:T(8,128)(2,1)}), bf16[16,2,16,1024]{3,2,1,0:T(8,128)(2,1)}, u32[]{:S(2)}, u32[]{:S(2)}) async-start(bf16[16,2,16,1024]{3,2,1,0:T(8,128)(2,1)} %spread.1), calls=%async_computation.2 | async-start | bytes 2097152 | tf_op jit(solution)/shard_map/all_to_all | solution.py:291

commit v4 on v3

--- a/solution.py
+++ b/solution.py
@@ -47,12 +47,11 @@
         ref[at + s : at + s + 64, to : to + TB] = wendland(left[s : s + 64], right) * kept.astype(F32)
 
 
-def cols_kernel(lengths, pattern, blocks, coords, inverses, cov_cols, inverse):
+def cols_kernel(lengths, pattern, blocks, coords, cov_cols):
     col_tile = place()[1]
     left = as_columns(sites(col_tile, lengths, blocks, coords))
     for p in range(2):
         put(cov_cols, 0, p * TB, left, sites(p, lengths, blocks, coords), pattern[col_tile, p])
-        inverse[p] = bf(inverses[p])
 
 
 def panels_kernel(row_tiles_n, row_count):
@@ -98,7 +97,7 @@
     def body(earlier, out, staged, sems, out_sems):
         row, col = place()
         count = out.shape[0]
-        held = jnp.logical_and(row // 2 == col % count // 2, col >= count + 2)
+        held = jnp.logical_and(row // 2 == col % count // 2, col >= count)
         start = jnp.where(held, 2 * count, 0) + col % 2 * count
         each = count // parts
         steps = [n * each for n in range(parts)]
@@ -113,22 +112,12 @@
     return body
 
 
-def spread_kernel(scattered, exchanged, planed, out, piece, sems, out_sems):
+def spread_kernel(scattered, exchanged, out, piece, sems, out_sems):
     _, col = place()
     count = out.shape[0]
     core = col % 2
-    clash = col // 2 == count // 2
-
-    @pl.when(clash)
-    def _():
-        for copy in fetch([(planed.at[h], piece.at[h]) for h in range(2)], sems):
-            copy.wait()
-
-    @pl.when(jnp.logical_not(clash))
-    def _():
-        for copy in fetch([(scattered.at[col % count], piece.at[core]), (exchanged.at[0], piece.at[1 - core])], sems):
-            copy.wait()
-
+    for copy in fetch([(scattered.at[col % count], piece.at[core]), (exchanged.at[0], piece.at[1 - core])], sems):
+        copy.wait()
     for copy in fetch([(piece, out.at[n]) for n in range(count)], out_sems):
         copy.wait()
 
@@ -150,14 +139,19 @@
 
 def rows_kernel(chunk):
     def body(
-        own, other, earlier, cov_rows_in, cov_first_in, inverse_in, first, second, first_tile,
-        panels, rows, cov_rows, cov_first, inverse, sems,
+        own, other, earlier, cov_rows_in, cov_first_in, inverses_in, first_out, second_out, first_tile_out, inverse_out,
+        panels, rows, cov_rows, cov_first, inverses, first, second, first_tile, inverse, sems, out_sems,
     ):
         steps = [pl.ds(s, chunk) for s in range(0, rows.shape[0], chunk)]
-        pairs = panel_parts(own, other, panels) + [(cov_first_in, cov_first), (inverse_in, inverse)]
+        pairs = panel_parts(own, other, panels) + [(inverses_in, inverses), (cov_first_in, cov_first)]
         for at in steps:
             pairs += [(earlier.at[at], rows.at[at]), (cov_rows_in.at[at], cov_rows.at[at])]
         copies = fetch(pairs, sems)
+        outs = []
+
+        def put_out(source, to):
+            outs.extend(fetch([(source, to)], out_sems.at[pl.ds(len(outs), 1)]))
+
         for copy in copies[:4]:
             copy.wait()
         zero = panels[0].reshape(TB, -1)
@@ -165,16 +159,23 @@
         tile = dot_t(one, zero)
         for copy in copies[4:6]:
             copy.wait()
+        inverse[...] = bf(inverses[...])
+        put_out(inverse, inverse_out)
         tile = times_inverse(cov_first[...] - tile, inverse[0])
         first_tile[...] = tile
+        put_out(first_tile, first_tile_out)
         for n, at in enumerate(steps):
             for copy in copies[6 + 2 * n : 8 + 2 * n]:
                 copy.wait()
             block = rows[at]
             got = times_inverse(cov_rows[at, :TB] - dot_t(block, zero), inverse[0])
             first[at] = got
+            put_out(first.at[at], first_out.at[at])
             rest = cov_rows[at, TB:] - dot_t(block, one) - dot_t(got, tile)
             second[at] = times_inverse(rest, inverse[1])
+            put_out(second.at[at], second_out.at[at])
+        for copy in outs:
+            copy.wait()
 
     return body
 
@@ -248,28 +249,24 @@
     )(halves)
     scattered = lax.all_to_all(mine, "row", 0, 0)
     col_index = lax.axis_index("col")
-    first_col = row_count // 2
-    to_row = jnp.clip(col_index - first_col, 0, row_count - 1)
-    planed = lax.dynamic_slice_in_dim(halves.reshape(2, 2, row_count, half, width)[1], to_row, 1, 1)
-    planed = lax.ppermute(
-        planed,
-        ("row", "col"),
-        [(t * col_count + first_col + r, r * col_count + row_count + t) for t in range(2) for r in range(row_count)],
-    )
     (cov_schur,) = call(
         schur_kernel(row_tiles_n, row_count),
         [jax.ShapeDtypeStruct((rows_n, TB), F32)],
         [SM, SM, SM, VM],
         name="schur",
     )(lengths, pattern, blocks, coords)
-    cov_cols, inverse = call(
-        cols_kernel,
-        [jax.ShapeDtypeStruct((TB, 2 * TB), F32), jax.ShapeDtypeStruct((2, TB, TB), BF16)],
-        [SM, SM, SM, VM, VM],
-        name="cols",
-    )(lengths, pattern, blocks, coords, inverses)
+    (cov_cols,) = call(
+        cols_kernel, [jax.ShapeDtypeStruct((TB, 2 * TB), F32)], [SM, SM, SM, VM], name="cols"
+    )(lengths, pattern, blocks, coords)
     scattered, cov_schur, cov_cols, later = lax.optimization_barrier((scattered, cov_schur, cov_cols, lengths))
-    own = lax.all_to_all(jnp.broadcast_to(scattered[:2], both), "row", 0, 0)
+    panel_piece = scattered[:2]
+    passed = lax.ppermute(
+        panel_piece,
+        ("row", "col"),
+        [(r * col_count + row_count + 2 + k, r * col_count + row_count + k) for r in range(row_count) for k in range(2)],
+    )
+    panel_piece = jnp.where(col_index // 2 == row_count // 2, passed, panel_piece)
+    own = lax.all_to_all(jnp.broadcast_to(panel_piece, both), "row", 0, 0)
     partner = [(c, c ^ 1) for c in range(col_count)]
     theirs = lax.dynamic_slice_in_dim(scattered, (col_index ^ 1) % row_count, 1, 0)
     exchanged = lax.ppermute(theirs, "col", partner)
@@ -282,11 +279,11 @@
     spread = call(
         spread_kernel,
         jax.ShapeDtypeStruct(both, BF16),
-        [HB] * 3,
+        [HB] * 2,
         HB,
         scratch_shapes=[pltpu.VMEM(both[1:], BF16), dma((2,)), dma((row_count,))],
         name="spread",
-    )(scattered, exchanged, planed.reshape(both[1:]))
+    )(scattered, exchanged)
     own, spread, cov_rows = lax.optimization_barrier((own, spread, cov_rows))
     column = lax.all_to_all(spread, "row", 0, 0)
     other = lax.ppermute(own, "col", partner)
@@ -298,19 +295,22 @@
     tall = pltpu.VMEM((rows_n, TB), BF16)
     whole = pltpu.VMEM(earlier.shape, BF16)
     block = pltpu.VMEM((rows_n, TB), F32)
-    first, second, first_tile = call(
+    first, second, first_tile, inverse = call(
         rows_kernel(chunk),
         [
             jax.ShapeDtypeStruct((rows_n, TB), BF16),
             jax.ShapeDtypeStruct((rows_n, TB), BF16),
             jax.ShapeDtypeStruct((TB, TB), BF16),
+            jax.ShapeDtypeStruct((2, TB, TB), BF16),
         ],
         [HB] * 6,
+        [HB] * 4,
         scratch_shapes=[
-            panels, whole, pltpu.VMEM((rows_n, 2 * TB), F32), pltpu.VMEM((TB, TB), F32), pair, dma((6 + 2 * count,)),
+            panels, whole, pltpu.VMEM((rows_n, 2 * TB), F32), pltpu.VMEM((TB, TB), F32),
+            pltpu.VMEM((2, TB, TB), F32), tall, tall, square, pair, dma((6 + 2 * count,)), dma((2 + 2 * count,)),
         ],
         name="rows",
-    )(own, other, earlier, cov_rows, cov_first, inverse)
+    )(own, other, earlier, cov_rows, cov_first, inverses)
     return call(
         tail_kernel(chunk),
         jax.ShapeDtypeStruct((rows_n, TB), F32),

time: 85.5 us -> 82.4 us (0.964)
  the two profiles are of different devices: /device:TPU:128 before, /device:TPU:256 now
where the time goes in v4:
time: 82.4 us; the launch traced here: 81.9 us
  Pallas kernels  36 us (44%)
  waiting for transfers between devices  22.8 us (28%)
  starting transfers between devices  21.1 us (26%)
  local copies, waits for them, and re-layouts  1.75 us (2%)
    all_to_all x1, waiting for transfers between devices, steps(): column = lax.all_to_all(spread, 'row', 0, 0)  10.5 us
    pallas_call x1, Pallas kernels, steps(): call(rows_kernel(chunk), [jax.ShapeDtypeStruct((rows_n, TB), BF16), jax.S...  8.99 us
    pallas_call x1, Pallas kernels, steps(): call(tail_kernel(chunk), jax.ShapeDtypeStruct((rows_n, TB), F32), [HB] *...  8.11 us
    all_to_all x1, starting transfers between devices, steps(): scattered = lax.all_to_all(mine, 'row', 0, 0)  7.05 us
    pallas_call x1, Pallas kernels, steps(): call(panels_kernel(row_tiles_n, row_count), [jax.ShapeDtypeStruct((rows_n...  6.94 us
    ppermute x1, waiting for transfers between devices, steps(): lax.ppermute(panel_piece, ('row', 'col'), [(r * col_count + row_count + 2...  4.84 us
    all_to_all x1, starting transfers between devices, steps(): column = lax.all_to_all(spread, 'row', 0, 0)  4.53 us
    all_to_all x1, starting transfers between devices, steps(): own = lax.all_to_all(jnp.broadcast_to(panel_piece, both), 'row', 0, 0)  4.35 us
  transfers between devices with their start and end apart: 6, of which 4 were waited for; matrix products, arithmetic and copies ran while one was open for 0% of the time, Pallas kernels for 32%

profile of v4, /device:TPU:256, one launch (start us, length us, event | category | flops | bytes accessed | tf_op | source)
XLA Modules:
  0.0 81.9 jit_solution(14715773901236122444)
XLA Ops:
  0.0 1.8 %pack.1 = bf16[16,16,1024]{2,1,0:T(8,128)(2,1)} custom-call(bf16[64,16,1024]{2,1,0:T(8,128)(2,1)} %bitcast.1), custom_call_target="tpu_custom_call" | custom-call | tf_op jit(solution)/shard_map/pack/pallas_call | solution.py:242
  1.8 7.0 %all-to-all-start = ((bf16[16,16,1024]{2,1,0:T(8,128)(2,1)}), bf16[16,16,1024]{2,1,0:T(8,128)(2,1)S(1)}, u32[]{:S(2)}, u32[]{:S(2)}) async-start(bf16[16,16,1024]{2,1,0:T(8,128)(2,1)} %pack.1), calls=%async_computation | async-start | bytes 1048576 | tf_op jit(solution)/shard_map/all_to_all | solution.py:250
  8.8 4.2 %schur.1.cov_schur_in = f32[1024,512]{1,0:T(8,128)} custom-call(f32[3]{0:T(128)} %lengths.4, s32[32,32]{1,0:T(8,128)} %pattern.5, s32[32]{0:T(128)} %blocks.5, f32[3,16384]{1,0:T(4,128)} %coords.5), custom_call_target="tpu_custom_call" | custom-call | tf_op jit(solution)/shard_map/schur/pallas_call | solution.py:252
  13.0 4.1 %cols.1.cov_cols_in = f32[512,1024]{1,0:T(8,128)} custom-call(f32[3]{0:T(128)} %lengths.4, s32[32,32]{1,0:T(8,128)} %pattern.5, s32[32]{0:T(128)} %blocks.5, f32[3,16384]{1,0:T(4,128)} %coords.5), custom_call_target="tpu_custom_call" | custom-call | tf_op jit(solution)/shard_map/cols/pallas_call | solution.py:258
  17.1 3.2 %all-to-all-done.scattered = bf16[16,16,1024]{2,1,0:T(8,128)(2,1)S(1)} async-done(((bf16[16,16,1024]{2,1,0:T(8,128)(2,1)}), bf16[16,16,1024]{2,1,0:T(8,128)(2,1)S(1)}, u32[]{:S(2)}, u32[]{:S(2)}) %all-to-all-start) | async-done | bytes 524320 | tf_op jit(solution)/shard_map/all_to_all | solution.py:250
  20.4 0.0 copy-start
  20.4 1.3 %collective-permute-start = (bf16[2,16,1024]{2,1,0:T(8,128)(2,1)S(1)}, bf16[2,16,1024]{2,1,0:T(8,128)(2,1)S(1)}, u32[]{:S(2)}, u32[]{:S(2)}) collective-permute-start(bf16[2,16,1024]{2,1,0:T(8,128)(2,1)S(1)} %slice.3), channel_id=1, source_target_pairs={{18,16},{19,17},{50,48},{51,49},{82,80},{83,81},{114,112},{115,113... | collective-permute-start | bytes 196616 | tf_op jit(solution)/shard_map/ppermute | solution.py:263
  21.7 4.8 %collective-permute-done = bf16[2,16,1024]{2,1,0:T(8,128)(2,1)S(1)} collective-permute-done((bf16[2,16,1024]{2,1,0:T(8,128)(2,1)S(1)}, bf16[2,16,1024]{2,1,0:T(8,128)(2,1)S(1)}, u32[]{:S(2)}, u32[]{:S(2)}) %collective-permute-start) | collective-permute-done | bytes 65568 | tf_op jit(solution)/shard_map/ppermute | solution.py:263
  26.6 1.1 %broadcast_in_dim.3 = bf16[16,2,16,1024]{3,2,1,0:T(8,128)(2,1)} broadcast(bf16[2,16,1024]{2,1,0:T(8,128)(2,1)S(1)} %broadcast_select_fusion), dimensions={1,2,3} | broadcast | bytes 1114112 | tf_op jit(solution)/shard_map/broadcast_in_dim | solution.py:269
  27.7 4.4 %all-to-all-start.1 = ((bf16[16,2,16,1024]{3,2,1,0:T(8,128)(2,1)}), bf16[16,2,16,1024]{3,2,1,0:T(8,128)(2,1)}, u32[]{:S(2)}, u32[]{:S(2)}) async-start(bf16[16,2,16,1024]{3,2,1,0:T(8,128)(2,1)} %broadcast_in_dim.3), calls=%async_computation.1 | async-start | bytes 2097152 | tf_op jit(solution)/shard_map/all_to_all | solution.py:269
  32.1 1.9 %collective-permute-start.1 = (bf16[1,16,1024]{2,1,0:T(8,128)(2,1)S(1)}, bf16[1,16,1024]{2,1,0:T(8,128)(2,1)S(1)}, u32[]{:S(2)}, u32[]{:S(2)}) collective-permute-start(bf16[1,16,1024]{2,1,0:T(8,128)(2,1)S(1)} %constant_dynamic-slice_fusion), channel_id=1, source_target_pairs={{0,1},{1,0},{2,3},{3,2},{4,5},{5,4},{6,7},{7,6},{8,9},{9,8},{10,11... | collective-permute-start | bytes 98312 | tf_op jit(solution)/shard_map/ppermute | solution.py:272
  34.0 6.9 %panels.1 = (f32[1024,1024]{1,0:T(8,128)}, f32[512,512]{1,0:T(8,128)}) custom-call(f32[3]{0:T(128)} %lengths.4, s32[32,32]{1,0:T(8,128)} %pattern.5, s32[32]{0:T(128)} %blocks.5, f32[3,16384]{1,0:T(4,128)} %coords.5), custom_call_target="tpu_custom_call" | custom-call | tf_op jit(solution)/shard_map/panels/pallas_call | solution.py:273
  40.9 0.0 collective-permute-done.1.exchanged
  40.9 0.0 copy-done
  40.9 0.0 copy-start.1
  41.0 0.6 copy-done.1
  41.6 1.9 %spread.1 = bf16[16,2,16,1024]{3,2,1,0:T(8,128)(2,1)} custom-call(bf16[16,16,1024]{2,1,0:T(8,128)(2,1)} %copy-done, bf16[1,16,1024]{2,1,0:T(8,128)(2,1)} %copy-done.1), custom_call_target="tpu_custom_call" | custom-call | tf_op jit(solution)/shard_map/spread/pallas_call | solution.py:279
  43.4 4.2 %all-to-all-done.1.own = bf16[16,2,16,1024]{3,2,1,0:T(8,128)(2,1)} async-done(((bf16[16,2,16,1024]{3,2,1,0:T(8,128)(2,1)}), bf16[16,2,16,1024]{3,2,1,0:T(8,128)(2,1)}, u32[]{:S(2)}, u32[]{:S(2)}) %all-to-all-start.1) | async-done | bytes 1048608 | tf_op jit(solution)/shard_map/all_to_all | solution.py:269
  47.6 1.9 %collective-permute-start.2 = (bf16[16,2,16,1024]{3,2,1,0:T(8,128)(2,1)}, bf16[16,2,16,1024]{3,2,1,0:T(8,128)(2,1)}, u32[]{:S(2)}, u32[]{:S(2)}) collective-permute-start(bf16[16,2,16,1024]{3,2,1,0:T(8,128)(2,1)} %all-to-all-done.1.own), channel_id=1, source_target_pairs={{0,1},{1,0},{2,3},{3,2},{4,5},{5,4},{6,7},{7,6},{8,9},{9,8},{10,11... | collective-permute-start | bytes 3145736 | tf_op jit(solution)/shard_map/ppermute | solution.py:289
  49.6 4.5 %all-to-all-start.2 = ((bf16[16,2,16,1024]{3,2,1,0:T(8,128)(2,1)}), bf16[16,2,16,1024]{3,2,1,0:T(8,128)(2,1)}, u32[]{:S(2)}, u32[]{:S(2)}) async-start(bf16[16,2,16,1024]{3,2,1,0:T(8,128)(2,1)} %spread.1), calls=%async_computation.2 | async-start | bytes 2097152 | tf_op jit(solution)/shard_map/all_to_all | solution.py:288
  54.1 0.0 collective-permute-done.2.other
  54.1 9.0 %rows.1 = (bf16[1024,512]{1,0:T(8,128)(2,1)}, bf16[1024,512]{1,0:T(8,128)(2,1)}, bf16[512,512]{1,0:T(8,128)(2,1)}, bf16[2,512,512]{2,1,0:T(8,128)(2,1)}) custom-call(bf16[16,2,16,1024]{3,2,1,0:T(8,128)(2,1)} %all-to-all-done.1.own, bf16[16,2,16,1024]{3,2,1,0:T(8,128)(2,1)} %collective-permute-done.2.other, bf16[1024,1024]{1,0:T(8,128)(2,1)} %earlier.3, ...), custom_call_target="tpu_custom_call" | custom-call | tf_op jit(solution)/shard_map/rows/pallas_call | solution.py:298
  63.1 10.5 %all-to-all-done.2.column_in = bf16[16,2,16,1024]{3,2,1,0:T(8,128)(2,1)} async-done(((bf16[16,2,16,1024]{3,2,1,0:T(8,128)(2,1)}), bf16[16,2,16,1024]{3,2,1,0:T(8,128)(2,1)}, u32[]{:S(2)}, u32[]{:S(2)}) %all-to-all-start.2) | async-done | bytes 1048608 | tf_op jit(solution)/shard_map/all_to_all | solution.py:288
  73.6 8.1 %tail.1 = f32[1024,512]{1,0:T(8,128)} custom-call(bf16[16,2,16,1024]{3,2,1,0:T(8,128)(2,1)} %all-to-all-done.2.column_in, bf16[16,2,16,1024]{3,2,1,0:T(8,128)(2,1)} %all-to-all-done.1.own, bf16[16,2,16,1024]{3,2,1,0:T(8,128)(2,1)} %collective-permute-done.2.other, bf16[1024,1024]{1,0:T(8,128)(2,1)} %earlier.3, f32[1024,512]{1,0:T(8,128)} %schur.1.cov_schur_in, ...), custom_call_target="tpu_custom_call" | custom-call | tf_op jit(solution)/shard_map/tail/pallas_call | solution.py:314
  (3 shorter events, 0.0 us)
Async XLA Ops:
  1.8 18.6 %all-to-all-start = ((bf16[16,16,1024]{2,1,0:T(8,128)(2,1)}), bf16[16,16,1024]{2,1,0:T(8,128)(2,1)S(1)}, u32[]{:S(2)}, u32[]{:S(2)}) async-start(bf16[16,16,1024]{2,1,0:T(8,128)(2,1)} %pack.1), calls=%async_computation | async-start | bytes 1048576 | tf_op jit(solution)/shard_map/all_to_all | solution.py:250
  20.4 20.6 %copy-start = (bf16[16,16,1024]{2,1,0:T(8,128)(2,1)}, bf16[16,16,1024]{2,1,0:T(8,128)(2,1)S(1)}, u32[]{:S(2)}) copy-start(bf16[16,16,1024]{2,1,0:T(8,128)(2,1)S(1)} %all-to-all-done.scattered) | copy-start | bytes 1572868
  20.4 6.2 %collective-permute-start = (bf16[2,16,1024]{2,1,0:T(8,128)(2,1)S(1)}, bf16[2,16,1024]{2,1,0:T(8,128)(2,1)S(1)}, u32[]{:S(2)}, u32[]{:S(2)}) collective-permute-start(bf16[2,16,1024]{2,1,0:T(8,128)(2,1)S(1)} %slice.3), channel_id=1, source_target_pairs={{18,16},{19,17},{50,48},{51,49},{82,80},{83,81},{114,112},{115,113... | collective-permute-start | bytes 196616 | tf_op jit(solution)/shard_map/ppermute | solution.py:263
  27.7 20.0 %all-to-all-start.1 = ((bf16[16,2,16,1024]{3,2,1,0:T(8,128)(2,1)}), bf16[16,2,16,1024]{3,2,1,0:T(8,128)(2,1)}, u32[]{:S(2)}, u32[]{:S(2)}) async-start(bf16[16,2,16,1024]{3,2,1,0:T(8,128)(2,1)} %broadcast_in_dim.3), calls=%async_computation.1 | async-start | bytes 2097152 | tf_op jit(solution)/shard_map/all_to_all | solution.py:269
  32.1 8.9 %collective-permute-start.1 = (bf16[1,16,1024]{2,1,0:T(8,128)(2,1)S(1)}, bf16[1,16,1024]{2,1,0:T(8,128)(2,1)S(1)}, u32[]{:S(2)}, u32[]{:S(2)}) collective-permute-start(bf16[1,16,1024]{2,1,0:T(8,128)(2,1)S(1)} %constant_dynamic-slice_fusion), channel_id=1, source_target_pairs={{0,1},{1,0},{2,3},{3,2},{4,5},{5,4},{6,7},{7,6},{8,9},{9,8},{10,11... | collective-permute-start | bytes 98312 | tf_op jit(solution)/shard_map/ppermute | solution.py:272
  40.9 0.6 copy-start.1
  47.6 6.5 %collective-permute-start.2 = (bf16[16,2,16,1024]{3,2,1,0:T(8,128)(2,1)}, bf16[16,2,16,1024]{3,2,1,0:T(8,128)(2,1)}, u32[]{:S(2)}, u32[]{:S(2)}) collective-permute-start(bf16[16,2,16,1024]{3,2,1,0:T(8,128)(2,1)} %all-to-all-done.1.own), channel_id=1, source_target_pairs={{0,1},{1,0},{2,3},{3,2},{4,5},{5,4},{6,7},{7,6},{8,9},{9,8},{10,11... | collective-permute-start | bytes 3145736 | tf_op jit(solution)/shard_map/ppermute | solution.py:289
  49.6 24.0 %all-to-all-start.2 = ((bf16[16,2,16,1024]{3,2,1,0:T(8,128)(2,1)}), bf16[16,2,16,1024]{3,2,1,0:T(8,128)(2,1)}, u32[]{:S(2)}, u32[]{:S(2)}) async-start(bf16[16,2,16,1024]{3,2,1,0:T(8,128)(2,1)} %spread.1), calls=%async_computation.2 | async-start | bytes 2097152 | tf_op jit(solution)/shard_map/all_to_all | solution.py:288
